TPU v7x, 128 devices: a whole 4x4x4 slice. The times are simulated.
128 devices in a mesh: blk: 32 (over y, z, x_hi), rhs: 4 (over x_lo, core).
Axes of the slice: x: 4 (x_hi: 2, x_lo: 2; x = x_hi * 2 + x_lo), y: 4, z: 4, core: 2. Of those that a mesh axis runs over, the one named last changes fastest.
Arguments:
- strips: float32 [256, 25, 128, 128], P('blk'), may hold values from -0.109375 to 0.109375
- near_cols: int32 [256, 25], P('blk'), may hold values from 0 to 255, as said below
- vector_block: float32 [32768, 2048], P(('blk', 'rhs')), may hold values from -6 to 6
- basis: float32 [4, 32768, 2048], P(None, ('blk', 'rhs')), may hold values from -0.03125 to 0.03125
Outputs:
- new_block: float32 [32768, 2048], P(('blk', 'rhs'))
- coeffs: float32 [4, 16, 128, 128], replicated
- factor: float32 [16, 128, 128], replicated
Inputs may be any that keep to these rules, and one draw needn't show every extreme that they name: `near_cols`: each row block has 25 distinct column blocks; slot 0 is the row block itself; every column block lies within 24 blocks of its row block, counted cyclically modulo 256, and some row block has a column block exactly 24 blocks above it.
All inputs are finite; a program needn't handle non-finite values.
Results may differ from a plain program's by a relative error of at most 0.0003.
Values sent between devices are 32-bit elements; how exact they have to be, the bound alone decides.
A program may use at most 256 MiB of HBM per device.

v0:
```python
import jax
import jax.numpy as jnp
from jax import lax
from jax.sharding import PartitionSpec as P

HOPS = 3
GROUP = 128


HIGHEST = lax.Precision.HIGHEST


def from_behind(value, axis, by):
    devices = lax.axis_size(axis)
    return lax.ppermute(value, axis, [(i, (i + by) % devices) for i in range(devices)])


def apply_strips(window, positions, strips):
    block = strips.shape[2]
    width = window.shape[1]
    pieces = window.reshape(window.shape[0] // block, block, width)
    chosen = pieces[positions]
    result = jnp.einsum("ikab,ikbc->iac", strips, chosen, precision=HIGHEST)
    return result.reshape(strips.shape[0] * block, width)


def local(strips, near_cols, vector_block, basis):
    local_blocks = strips.shape[0]
    total_blocks = local_blocks * lax.axis_size("blk")
    row_form = lax.all_to_all(vector_block, "rhs", split_axis=1, concat_axis=0, tiled=True)
    gathered = []
    for offset in range(-HOPS, HOPS + 1):
        if offset == 0:
            gathered.append(row_form)
        else:
            gathered.append(from_behind(row_form, "blk", -offset))
    window = jnp.concatenate(gathered, axis=0)
    first_block = (lax.axis_index("blk") - HOPS) * local_blocks
    positions = jnp.mod(near_cols - first_block, total_blocks)
    image = apply_strips(window, positions, strips)
    column_form = lax.all_to_all(image, "rhs", split_axis=0, concat_axis=1, tiled=True)
    local_rows, width = column_form.shape
    groups = width // GROUP
    grouped = column_form.reshape(local_rows, groups, GROUP)
    basis_grouped = basis.reshape(basis.shape[0], local_rows, groups, GROUP)
    partial_value = jnp.einsum("mnga,ngb->mgab", basis_grouped, grouped, precision=HIGHEST)
    coeffs = lax.psum(partial_value, ("blk", "rhs"))
    residual = grouped - jnp.einsum("mnga,mgab->ngb", basis_grouped, coeffs, precision=HIGHEST)
    local_gram = jnp.einsum("nga,ngb->gab", residual, residual, precision=HIGHEST)
    gram = lax.psum(local_gram, ("blk", "rhs"))
    factor = jnp.linalg.cholesky(gram)
    solved = jax.scipy.linalg.solve_triangular(
        factor, jnp.transpose(residual, (1, 2, 0)), lower=True
    )
    new_block = jnp.transpose(solved, (2, 0, 1)).reshape(local_rows, width)
    return (new_block, coeffs, factor)


def solution(mesh):
    placed = (
        P("blk", None, None, None),
        P("blk", None),
        P(("blk", "rhs"), None),
        P(None, ("blk", "rhs"), None),
    )
    return jax.shard_map(
        local,
        mesh=mesh,
        in_specs=placed,
        out_specs=(P(("blk", "rhs"), None), P(), P()),
        check_vma=False,
    )
```

profile of v0, /device:TPU:1, one launch (start us, length us, event | category | flops | bytes accessed | tf_op | source)
XLA Modules:
  0.0 1048.3 jit_solution(446795296465004191)
XLA Ops:
  7.2 0.0 copy-start.2
  7.2 0.0 all-reduce.3.cloned.1.call-start
  7.2 1.9 copy.36
  9.2 29.2 %all_to_all.35 = f32[256,4,512]{0,2,1:T(8,128)} all-to-all(f32[256,4,512]{0,2,1:T(8,128)S(1)} %bitcast.75), channel_id=1, replica_groups=mesh['blk'=32,'rhs'=4] {'rhs'}, dimensions={1} | all-to-all | bytes 4194304 | tf_op jit(solution)/shard_map/all_to_all | solution.py:30
  38.4 1.9 copy.37
  40.3 4.3 collective-permute-start
  44.6 1.6 collective-permute-start.1
  46.2 1.3 collective-permute-start.2
  47.5 5.9 collective-permute-start.3
  53.4 0.0 collective-permute-start.4
  53.4 41.7 %collective-permute-done = f32[1024,512]{1,0:T(8,128)S(1)} collective-permute-done((f32[1024,512]{1,0:T(8,128)S(1)}, f32[1024,512]{1,0:T(8,128)S(1)}, u32[]{:S(2)}, u32[]{:S(2)}) %collective-permute-start) | collective-permute-done | bytes 2097184 | tf_op jit(solution)/shard_map/ppermute | solution.py:15
  95.2 0.0 copy-start.1
  95.2 1.3 copy-done.1
  96.5 2.4 collective-permute-start.5
  98.9 0.0 copy-done.2
  98.9 0.1 reshape.44
  99.0 3.1 constant_dynamic-update-slice_fusion.6
  102.1 83.8 %collective-permute-done.1 = f32[1024,512]{1,0:T(8,128)} collective-permute-done((f32[1024,512]{1,0:T(8,128)S(1)}, f32[1024,512]{1,0:T(8,128)}, u32[]{:S(2)}, u32[]{:S(2)}) %collective-permute-start.1) | collective-permute-done | bytes 2097184 | tf_op jit(solution)/shard_map/ppermute | solution.py:15
  185.9 3.1 constant_dynamic-update-slice_fusion.5
  189.0 0.0 collective-permute-done.2
  189.0 3.1 constant_dynamic-update-slice_fusion.4
  192.0 1.5 constant_dynamic-update-slice_fusion.3
  193.6 0.0 collective-permute-done.3
  193.6 3.1 constant_dynamic-update-slice_fusion.2
  196.6 0.0 collective-permute-done.4
  196.6 3.1 constant_dynamic-update-slice_fusion.1
  199.7 48.1 %collective-permute-done.5 = f32[1024,512]{1,0:T(8,128)} collective-permute-done((f32[1024,512]{1,0:T(8,128)S(1)}, f32[1024,512]{1,0:T(8,128)}, u32[]{:S(2)}, u32[]{:S(2)}) %collective-permute-start.5) | collective-permute-done | bytes 2097184 | tf_op jit(solution)/shard_map/ppermute | solution.py:15
  247.8 3.1 constant_dynamic-update-slice_fusion
  250.9 24.7 %gather_fusion = f32[200,128,512]{2,1,0:T(8,128)} fusion(f32[56,128,512]{2,1,0:T(8,128)} %bitcast.3, s32[1024]{0:T(1024)S(1)} %pad_clamp_fusion), kind=kCustom, calls=%fused_computation | custom fusion | bytes 104858400 | tf_op jit(solution)/shard_map/gather | solution.py:22
  275.7 33.5 %fusion.16 = f32[8,512,128,1]{1,2,3,0:T(8,128)S(1)} fusion(f32[8,25,128,512]{3,2,1,0:T(8,128)} %bitcast.61, f32[8,25,128,128]{3,2,1,0:T(8,128)} %param.4), kind=kOutput, calls=%fused_computation.33 | convolution fusion | flops 20132659200 | bytes 67633152 | tf_op jit(solution)/shard_map/ikab,ikbc->iac/dot_general | solution.py:23
  309.2 32.9 %all_to_all.36 = f32[4,256,512]{2,1,0:T(8,128)} all-to-all(f32[4,256,512]{2,1,0:T(8,128)S(1)} %bitcast.64), channel_id=1, replica_groups=mesh['blk'=32,'rhs'=4] {'rhs'}, dimensions={0} | all-to-all | bytes 4194304 | tf_op jit(solution)/shard_map/all_to_all | solution.py:41
  342.1 1.9 copy.38
  344.1 0.0 copy-start
  344.1 11.5 %fusion.6 = f32[4,16,128,128]{2,3,0,1:T(8,128)} fusion(f32[256,16,128,1]{0,2,3,1:T(8,128)S(1)} %bitcast.62, f32[4,256,2048]{2,1,0:T(8,128)} %param.7), kind=kOutput, calls=%fused_computation.7 | convolution fusion | flops 3221225472 | bytes 14680064 | tf_op jit(solution)/shard_map/mnga,ngb->mgab/dot_general | solution.py:46
  355.6 0.0 all-reduce.3.cloned.1.call-update
  355.6 0.0 copy-done
  355.6 0.0 all-reduce.5.cloned.1.call-start
  355.7 164.1 %all-reduce.3.cloned.1.call-done = f32[4,16,128,128]{2,3,0,1:T(8,128)} async-done(((f32[4,16,128,128]{2,3,0,1:T(8,128)}), f32[4,16,128,128]{2,3,0,1:T(8,128)}) %all-reduce.3.cloned.1.call-update) | async-done | bytes 4194320 | tf_op jit(solution)/shard_map/psum | solution.py:47
  519.8 13.7 %bitcast_subtract_fusion = f32[256,16,128]{0,2,1:T(8,128)S(1)} fusion(f32[256,16,128]{0,2,1:T(8,128)} %bitcast.63, f32[4,16,128,128]{2,3,0,1:T(8,128)} %all-reduce.3.cloned.1.call-done, f32[4,256,2048]{2,1,0:T(8,128)} %param.7), kind=kOutput, calls=%fused_computation.8 | convolution fusion | flops 3221749760 | bytes 16777216 | tf_op jit(solution)/shard_map/mnga,mgab->ngb/dot_general | solution.py:48
  533.5 3.1 fusion.17
  536.6 0.0 all-reduce.5.cloned.1.call-update
  536.6 5.6 copy.46
  542.2 141.3 %all-reduce.5.cloned.1.call-done = f32[16,128,128]{1,2,0:T(8,128)} async-done(((f32[16,128,128]{1,2,0:T(8,128)}), f32[16,128,128]{1,2,0:T(8,128)}) %all-reduce.5.cloned.1.call-update) | async-done | bytes 1048592 | tf_op jit(solution)/shard_map/psum | solution.py:50
  683.5 1.6 copy.43
  685.0 2.3 fusion.14
  687.3 188.3 %custom-call.8 = f32[16,128,128]{2,1,0:T(8,128)S(1)} custom-call(f32[16,128,128]{2,1,0:T(8,128)} %fusion.14), custom_call_target="Cholesky" | custom-call | tf_op jit(solution)/shard_map/jit(cholesky)/cholesky | solution.py:51
  875.6 0.1 select_reduce_fusion
  875.7 0.1 compare_reduce_fusion
  875.9 1.5 select_bitcast_fusion
  877.4 157.9 %custom-call.9 = f32[16,1,128,128]{2,3,1,0:T(8,128)S(1)} custom-call(f32[16,1,128,128]{3,2,1,0:T(8,128)} %get-tuple-element.15), custom_call_target="InvertDiagBlocksLowerTriangular" | custom-call | tf_op jit(solution)/shard_map/jit(_solve_triangular)/vmap()/triangular_solve | solution.py:52
  1035.3 3.2 fusion.9
  1038.6 2.9 copy.45
  (4 shorter events, 0.1 us)
Async XLA Ops:
  7.2 91.7 %copy-start.2 = (s32[8,25]{1,0:T(8,128)S(1)}, s32[8,25]{1,0:T(8,128)}, u32[]{:S(2)}) copy-start(s32[8,25]{1,0:T(8,128)} %param.5) | copy-start | bytes 2404
  7.2 512.6 %all-reduce.3.cloned.1.call-start = ((), (), s32[]{:S(2)}) async-start(), calls=%async_computation.2 | async-start | bytes 8388608 | tf_op jit(solution)/shard_map/psum | solution.py:47
  40.3 54.8 %collective-permute-start = (f32[1024,512]{1,0:T(8,128)S(1)}, f32[1024,512]{1,0:T(8,128)S(1)}, u32[]{:S(2)}, u32[]{:S(2)}) collective-permute-start(f32[1024,512]{1,0:T(8,128)S(1)} %bitcast.65), channel_id=1, source_target_pairs={{0,12},{4,16},{8,20},{12,24},{16,28},{20,32},{24,36},{28,40},{32,4... | collective-permute-start | bytes 6291464 | tf_op jit(solution)/shard_map/ppermute | solution.py:15
  44.6 141.3 %collective-permute-start.1 = (f32[1024,512]{1,0:T(8,128)S(1)}, f32[1024,512]{1,0:T(8,128)}, u32[]{:S(2)}, u32[]{:S(2)}) collective-permute-start(f32[1024,512]{1,0:T(8,128)S(1)} %bitcast.66), channel_id=1, source_target_pairs={{0,8},{4,12},{8,16},{12,20},{16,24},{20,28},{24,32},{28,36},{32,40... | collective-permute-start | bytes 6291464 | tf_op jit(solution)/shard_map/ppermute | solution.py:15
  46.2 142.7 %collective-permute-start.2 = (f32[1024,512]{1,0:T(8,128)S(1)}, f32[1024,512]{1,0:T(8,128)}, u32[]{:S(2)}, u32[]{:S(2)}) collective-permute-start(f32[1024,512]{1,0:T(8,128)S(1)} %bitcast.67), channel_id=1, source_target_pairs={{0,4},{4,8},{8,12},{12,16},{16,20},{20,24},{24,28},{28,32},{32,36}... | collective-permute-start | bytes 6291464 | tf_op jit(solution)/shard_map/ppermute | solution.py:15
  47.5 146.0 %collective-permute-start.3 = (f32[1024,512]{1,0:T(8,128)S(1)}, f32[1024,512]{1,0:T(8,128)}, u32[]{:S(2)}, u32[]{:S(2)}) collective-permute-start(f32[1024,512]{1,0:T(8,128)S(1)} %bitcast.68), channel_id=1, source_target_pairs={{0,124},{4,0},{8,4},{12,8},{16,12},{20,16},{24,20},{28,24},{32,28}... | collective-permute-start | bytes 6291464 | tf_op jit(solution)/shard_map/ppermute | solution.py:15
  53.4 143.2 %collective-permute-start.4 = (f32[1024,512]{1,0:T(8,128)S(1)}, f32[1024,512]{1,0:T(8,128)}, u32[]{:S(2)}, u32[]{:S(2)}) collective-permute-start(f32[1024,512]{1,0:T(8,128)S(1)} %bitcast.69), channel_id=1, source_target_pairs={{0,120},{4,124},{8,0},{12,4},{16,8},{20,12},{24,16},{28,20},{32,24... | collective-permute-start | bytes 6291464 | tf_op jit(solution)/shard_map/ppermute | solution.py:15
  95.2 1.3 copy-start.1
  96.5 151.4 %collective-permute-start.5 = (f32[1024,512]{1,0:T(8,128)S(1)}, f32[1024,512]{1,0:T(8,128)}, u32[]{:S(2)}, u32[]{:S(2)}) collective-permute-start(f32[1024,512]{1,0:T(8,128)S(1)} %bitcast.70), channel_id=1, source_target_pairs={{0,116},{4,120},{8,124},{12,0},{16,4},{20,8},{24,12},{28,16},{32,2... | collective-permute-start | bytes 6291464 | tf_op jit(solution)/shard_map/ppermute | solution.py:15
  344.1 11.6 %copy-start = (f32[256,4,512]{0,2,1:T(8,128)}, f32[256,4,512]{0,2,1:T(8,128)S(1)}, u32[]{:S(2)}) copy-start(f32[256,4,512]{0,2,1:T(8,128)S(1)} %copy.38) | copy-start | bytes 6291460
  355.6 327.8 %all-reduce.5.cloned.1.call-start = ((), (), s32[]{:S(2)}) async-start(), calls=%async_computation.3 | async-start | bytes 2097152 | tf_op jit(solution)/shard_map/psum | solution.py:50
Sparse Core Ops, SparseCore 0:
  355.7 163.9 all-reduce.2
  536.7 146.7 all-reduce.4
where the time goes:
time: 1050 us
  waiting for transfers between devices  479 us (46%)
  other arithmetic  350 us (33%)
  matrix products  65.1 us (6%)
  blocking collectives  62.2 us (6%)
  local copies, waits for them, and re-layouts  61.9 us (6%)
  starting transfers between devices  15.6 us (1%)
  between operations  14.2 us (1%)
    another operation x4, other arithmetic, local(): factor = jnp.linalg.cholesky(gram)  189 us
    ppermute x6, waiting for transfers between devices, from_behind(): lax.ppermute(value, axis, [(i, (i + by) % devices) for i in range(devices)])  174 us
    psum x1, waiting for transfers between devices, local(): coeffs = lax.psum(partial_value, ('blk', 'rhs'))  164 us
    another operation x3, other arithmetic, local(): jax.scipy.linalg.solve_triangular(factor, jnp.transpose(residual, (1, 2,...  159 us
    psum x1, waiting for transfers between devices, local(): gram = lax.psum(local_gram, ('blk', 'rhs'))  141 us
    dot_general x1, matrix products, apply_strips(): result = jnp.einsum('ikab,ikbc->iac', strips, chosen, precision=HIGHEST)  33.5 us
    all_to_all x1, blocking collectives, local(): lax.all_to_all(image, 'rhs', split_axis=0, concat_axis=1, tiled=True)  32.9 us
    all_to_all x1, blocking collectives, local(): lax.all_to_all(vector_block, 'rhs', split_axis=1, concat_axis=0, tiled=True)  29.2 us
  transfers between devices with their start and end apart: 8, of which 5 were waited for; matrix products, arithmetic and copies ran while one was open for 2% of the time, Pallas kernels for 0%

commit v1 on v0

v1 whole, which is shorter than its diff:
```python
import functools

import jax
import jax.numpy as jnp
from jax import lax
from jax.experimental import pallas as pl
from jax.experimental.pallas import tpu as pltpu
from jax.sharding import PartitionSpec as P

HOPS = 3
GROUP = 128
MESH = pl.DeviceIdType.MESH
HIGHEST = lax.Precision.HIGHEST
BF16, F32 = jnp.bfloat16, jnp.float32
VMEM_SPEC = pl.BlockSpec(memory_space=pltpu.VMEM)


def split(value):
    high = value.astype(BF16)
    low = (value - high.astype(F32)).astype(BF16)
    return high, low


def dot1(a, b, ca, cb):
    return lax.dot_general(a, b, (((ca,), (cb,)), ((), ())), preferred_element_type=F32)


def dot3(a, b, ca, cb):
    ah, al = split(a)
    bh, bl = split(b)
    return dot1(ah, bh, ca, cb) + (dot1(ah, bl, ca, cb) + dot1(al, bh, ca, cb))


ORDERS = ((0, 1, 2), (1, 2, 0), (2, 0, 1))


def coordinates():
    blk, rhs = lax.axis_index("blk"), lax.axis_index("rhs")
    x = (blk % 2) * 2 + rhs // 2
    return (x, blk // 8, (blk // 2) % 4), rhs % 2


def device_of(place, core):
    x, y, z = place
    return {"blk": (y * 4 + z) * 2 + x // 2, "rhs": (x % 2) * 2 + core}


def moved(place, axis, by):
    at = list(place)
    at[axis] = (at[axis] + by) % 4
    return tuple(at)


def all_sum_kernel(shares, x_ref, out_ref, from_core, *rest):
    parts = len(shares)
    received, acc = rest[: 3 * parts], rest[3 * parts : 5 * parts]
    send_sem, recv_sem = rest[5 * parts :]
    place, core = coordinates()
    half = x_ref.shape[0] // 2
    partner = device_of(place, 1 - core)
    peers = [device_of(moved(place, axis, by), core) for axis in range(3) for by in (1, 2, 3)]

    barrier = pltpu.get_barrier_semaphore()
    for peer in [partner] + peers:
        pl.semaphore_signal(barrier, inc=1, device_id=peer, device_id_type=MESH)
    pl.semaphore_wait(barrier, 10)

    counter = [0]

    def copy(src, dst, device):
        at = counter[0]
        counter[0] += 1
        made = pltpu.make_async_remote_copy(
            src_ref=src, dst_ref=dst, send_sem=send_sem.at[at], recv_sem=recv_sem.at[at],
            device_id=device, device_id_type=MESH,
        )
        made.start()
        return made

    offsets, total = [], 0
    for share in shares:
        offsets.append(total)
        total += 64 * share
    mine, other = core * half, (1 - core) * half

    first = [
        copy(x_ref.at[pl.ds(other + offset, 64 * share)], from_core.at[pl.ds(offset, 64 * share)], partner)
        for offset, share in zip(offsets, shares)
    ]
    pending = []
    for part, (offset, share) in enumerate(zip(offsets, shares)):
        first[part].wait_recv()
        rows = pl.ds(offset, 64 * share)
        from_core[rows] = from_core[rows] + x_ref[pl.ds(mine + offset, 64 * share)]

    sources = [from_core.at[pl.ds(offset, 64 * share)] for offset, share in zip(offsets, shares)]
    for stage in range(3):
        copies = []
        for part, share in enumerate(shares):
            axis = ORDERS[part][stage]
            size = share * 4 ** (2 - stage)
            block = []
            for by in (1, 2, 3):
                to = (place[axis] + by) % 4
                block.append(copy(
                    sources[part].at[pl.ds(to * size, size)],
                    received[3 * part + stage].at[by - 1],
                    device_of(moved(place, axis, by), core),
                ))
            copies.append(block)
        for part, share in enumerate(shares):
            axis = ORDERS[part][stage]
            size = share * 4 ** (2 - stage)
            for made in copies[part]:
                made.wait_recv()
            got = received[3 * part + stage]
            value = sources[part][pl.ds(place[axis] * size, size)] + got[0] + got[1] + got[2]
            if stage < 2:
                acc[2 * part + stage][...] = value
                sources[part] = acc[2 * part + stage]
            else:
                sources[part] = value
        pending += [made for block in copies for made in block]

    starts = []
    for part, share in enumerate(shares):
        at = mine + offsets[part]
        for stage in range(3):
            at = at + place[ORDERS[part][stage]] * share * 4 ** (2 - stage)
        starts.append(at)
        out_ref[pl.ds(at, share)] = sources[part]
    for stage in (2, 1, 0):
        copies = []
        for part, share in enumerate(shares):
            axis = ORDERS[part][stage]
            size = share * 4 ** (2 - stage)
            at = mine + offsets[part]
            for before in range(stage + 1):
                at = at + place[ORDERS[part][before]] * share * 4 ** (2 - before)
            rows = out_ref.at[pl.ds(at, size)]
            for by in (1, 2, 3):
                copies.append(copy(rows, rows, device_of(moved(place, axis, by), core)))
        for made in copies:
            made.wait_recv()
        pending += copies
    rows = out_ref.at[pl.ds(mine, half)]
    last = copy(rows, rows, partner)
    last.wait_recv()
    for made in first + pending + [last]:
        made.wait_send()


def all_sum(value, shares, collective_id):
    rows = value.shape[0]
    scratch = [pltpu.VMEM((rows // 2, 128), F32)]
    for share in shares:
        scratch += [pltpu.VMEM((3, share * 4 ** (2 - stage), 128), F32) for stage in range(3)]
    for share in shares:
        scratch += [pltpu.VMEM((share * 4 ** (2 - stage), 128), F32) for stage in range(2)]
    copies = 2 * 9 * len(shares) + len(shares) + 1
    return pl.pallas_call(
        functools.partial(all_sum_kernel, shares),
        out_shape=jax.ShapeDtypeStruct(value.shape, F32),
        in_specs=[VMEM_SPEC],
        out_specs=VMEM_SPEC,
        scratch_shapes=scratch + [pltpu.SemaphoreType.DMA((copies,)), pltpu.SemaphoreType.DMA((copies,))],
        compiler_params=pltpu.CompilerParams(collective_id=collective_id, has_side_effects=True),
        name=f"all_sum_{rows}",
    )(value)


def coeffs_kernel(basis_ref, image_ref, out_ref):
    ih, il = split(image_ref[...])
    for m in range(basis_ref.shape[0]):
        bh, bl = split(basis_ref[m])
        out_ref[m, 0] = dot1(bh, ih, 0, 0) + (dot1(bh, il, 0, 0) + dot1(bl, ih, 0, 0))


def local_coeffs(basis, image):
    count, rows, width = basis.shape
    groups = width // GROUP
    return pl.pallas_call(
        coeffs_kernel,
        grid=(groups,),
        out_shape=jax.ShapeDtypeStruct((count, groups, GROUP, GROUP), F32),
        in_specs=[
            pl.BlockSpec((count, rows, GROUP), lambda g: (0, 0, g)),
            pl.BlockSpec((rows, GROUP), lambda g: (0, g)),
        ],
        out_specs=pl.BlockSpec((count, 1, GROUP, GROUP), lambda g: (0, g, 0, 0)),
        name="local_coeffs",
    )(basis, image)


def residual_kernel(basis_ref, image_ref, coeffs_ref, residual_ref, gram_ref):
    value = image_ref[...]
    for m in range(basis_ref.shape[0]):
        value = value - dot3(basis_ref[m], coeffs_ref[m, 0], 1, 0)
    residual_ref[...] = value
    gram_ref[0] = dot3(value, value, 0, 0)


def local_residual(basis, image, coeffs):
    count, rows, width = basis.shape
    groups = width // GROUP
    return pl.pallas_call(
        residual_kernel,
        grid=(groups,),
        out_shape=(
            jax.ShapeDtypeStruct((rows, width), F32),
            jax.ShapeDtypeStruct((groups, GROUP, GROUP), F32),
        ),
        in_specs=[
            pl.BlockSpec((count, rows, GROUP), lambda g: (0, 0, g)),
            pl.BlockSpec((rows, GROUP), lambda g: (0, g)),
            pl.BlockSpec((count, 1, GROUP, GROUP), lambda g: (0, g, 0, 0)),
        ],
        out_specs=(
            pl.BlockSpec((rows, GROUP), lambda g: (0, g)),
            pl.BlockSpec((1, GROUP, GROUP), lambda g: (g, 0, 0)),
        ),
        name="local_residual",
    )(basis, image, coeffs)


STEP = 32


def factor_kernel(gram_ref, residual_ref, new_ref, factor_ref, a_ref, b_ref):
    groups = gram_ref.shape[0]
    a_ref[...] = gram_ref[...]
    shape = (GROUP, GROUP)
    row_of = lax.broadcasted_iota(jnp.int32, shape, 0)
    lane_of = lax.broadcasted_iota(jnp.int32, shape, 1)
    eye = jnp.where(row_of == lane_of, 1.0, 0.0).astype(F32)
    b_ref[...] = jnp.broadcast_to(eye[None], (groups,) + shape)
    lane = lax.broadcasted_iota(jnp.int32, (1, 8, GROUP), 2)
    sub = lax.broadcasted_iota(jnp.int32, (1, 8, GROUP), 1)
    for block in range(GROUP // STEP):
        s = block * STEP
        o = (s + 64) % GROUP
        tiles = []
        for t in range(STEP // 8):
            rows = a_ref[:, s + 8 * t : s + 8 * t + 8, :]
            ones = jnp.where(lane == o + 8 * t + sub, 1.0, 0.0).astype(F32)
            tiles.append(jnp.where((lane >= s) & (lane < s + STEP), rows, ones))
        for j in range(STEP):
            at, within = j // 8, j % 8
            row = tiles[at][:, within : within + 1, :]
            scaled = row / tiles[at][:, within : within + 1, s + j : s + j + 1]
            for t in range(at, STEP // 8):
                column = tiles[t][:, :, s + j : s + j + 1]
                if t == at:
                    column = jnp.where(sub > within, column, 0.0)
                tiles[t] = tiles[t] - column * scaled
        for t in range(STEP // 8):
            diagonal = jnp.sum(jnp.where(lane == s + 8 * t + sub, tiles[t], 0.0), axis=2, keepdims=True)
            tiles[t] = tiles[t] * (1.0 / jnp.sqrt(diagonal))
        panel = jnp.concatenate(tiles, axis=1)
        for g in range(groups):
            inverse = panel[g, :, o : o + STEP]
            wa = jnp.dot(inverse, a_ref[g, s : s + STEP, :], precision=HIGHEST, preferred_element_type=F32)
            wb = jnp.dot(inverse, b_ref[g, s : s + STEP, :], precision=HIGHEST, preferred_element_type=F32)
            a_ref[g, s : s + STEP, :] = wa
            b_ref[g, s : s + STEP, :] = wb
            if s + STEP < GROUP:
                below = slice(s + STEP, GROUP)
                left = wa.T[s + STEP :, :]
                a_ref[g, below, :] = a_ref[g, below, :] - jnp.dot(left, wa, precision=HIGHEST, preferred_element_type=F32)
                b_ref[g, below, :] = b_ref[g, below, :] - jnp.dot(left, wb, precision=HIGHEST, preferred_element_type=F32)
    for g in range(groups):
        factor_ref[g] = jnp.where(row_of >= lane_of, a_ref[g].T, 0.0)
        inverse = jnp.where(row_of >= lane_of, b_ref[g], 0.0)
        columns = slice(g * GROUP, (g + 1) * GROUP)
        new_ref[:, columns] = dot3(residual_ref[:, columns], inverse, 1, 1)


def factor_and_solve(gram, residual):
    return pl.pallas_call(
        factor_kernel,
        out_shape=(jax.ShapeDtypeStruct(residual.shape, F32), jax.ShapeDtypeStruct(gram.shape, F32)),
        in_specs=[VMEM_SPEC, VMEM_SPEC],
        out_specs=(VMEM_SPEC, VMEM_SPEC),
        scratch_shapes=[pltpu.VMEM(gram.shape, F32), pltpu.VMEM(gram.shape, F32)],
        name="factor_and_solve",
    )(gram, residual)


def from_behind(value, axis, by):
    devices = lax.axis_size(axis)
    return lax.ppermute(value, axis, [(i, (i + by) % devices) for i in range(devices)])


def apply_strips(window, positions, strips):
    block = strips.shape[2]
    width = window.shape[1]
    pieces = window.reshape(window.shape[0] // block, block, width)
    chosen = pieces[positions]
    result = jnp.einsum("ikab,ikbc->iac", strips, chosen, precision=HIGHEST)
    return result.reshape(strips.shape[0] * block, width)


def apply_near_field(strips, near_cols, vector_block):
    local_blocks = strips.shape[0]
    total_blocks = local_blocks * lax.axis_size("blk")
    row_form = lax.all_to_all(vector_block, "rhs", split_axis=1, concat_axis=0, tiled=True)
    gathered = []
    for offset in range(-HOPS, HOPS + 1):
        if offset == 0:
            gathered.append(row_form)
        else:
            gathered.append(from_behind(row_form, "blk", -offset))
    window = jnp.concatenate(gathered, axis=0)
    first_block = (lax.axis_index("blk") - HOPS) * local_blocks
    positions = jnp.mod(near_cols - first_block, total_blocks)
    image = apply_strips(window, positions, strips)
    return lax.all_to_all(image, "rhs", split_axis=0, concat_axis=1, tiled=True)


def local(strips, near_cols, vector_block, basis):
    image = apply_near_field(strips, near_cols, vector_block)
    partial_coeffs = local_coeffs(basis, image)
    flat = partial_coeffs.reshape(-1, GROUP)
    coeffs = all_sum(flat, (24, 24, 16), 1).reshape(partial_coeffs.shape)
    residual, partial_gram = local_residual(basis, image, coeffs)
    gram = all_sum(partial_gram.reshape(-1, GROUP), (8, 8), 2).reshape(partial_gram.shape)
    new_block, factor = factor_and_solve(gram, residual)
    return (new_block, coeffs, factor)


def solution(mesh):
    placed = (
        P("blk", None, None, None),
        P("blk", None),
        P(("blk", "rhs"), None),
        P(None, ("blk", "rhs"), None),
    )
    return jax.shard_map(
        local,
        mesh=mesh,
        in_specs=placed,
        out_specs=(P(("blk", "rhs"), None), P(), P()),
        check_vma=False,
    )
```

time: 1050 us -> 512 us (0.49)
  other arithmetic: 350 us -> 0.71 us
  waiting for transfers between devices: 479 us -> 173 us
  Pallas kernels: 0 us -> 169 us
  matrix products: 65.1 us -> 33.5 us
  between operations: 14.2 us -> 0.69 us
    another operation x7 -> x0, other arithmetic: 348 us -> none  [the longest x4 189 us: local(): factor = jnp.linalg.cholesky(gram)]
    psum x2 -> x0, waiting for transfers between devices: 305 us -> none  [the longest x1 164 us: local(): coeffs = lax.psum(partial_value, ('blk', 'rhs'))]
    pallas_call x0 -> x5, Pallas kernels: none -> 169 us  [the longest x2 99 us: all_sum(): pl.pallas_call(functools.partial(all_sum_kernel, shares), out_shape=jax.S...]
    dot_general x3 -> x0, matrix products: 28.3 us -> none  [the longest x1 13.7 us: local(): jnp.einsum('mnga,mgab->ngb', basis_grouped, coeffs, precision=HIGHEST)]
    unnamed x15 -> x10, local copies, waits for them, and re-layouts: 28.6 us -> 24.9 us
  transfers between devices with their start and end apart: 8 -> 6, of which waited for: 5 -> 3; matrix products, arithmetic and copies ran while one was open for 2% -> 3% of each run, Pallas kernels for 0% -> 0%
where the time goes in v1:
time: 512 us; the launch traced here: 510 us
  waiting for transfers between devices  173 us (34%)
  Pallas kernels  169 us (33%)
  blocking collectives  62.1 us (12%)
  local copies, waits for them, and re-layouts  56.3 us (11%)
  matrix products  33.5 us (7%)
  starting transfers between devices  15.5 us (3%)
    ppermute x6, waiting for transfers between devices, from_behind(): lax.ppermute(value, axis, [(i, (i + by) % devices) for i in range(devices)])  173 us
    pallas_call x2, Pallas kernels, all_sum(): pl.pallas_call(functools.partial(all_sum_kernel, shares), out_shape=jax.S...  99 us
    pallas_call x1, Pallas kernels, factor_and_solve(): pl.pallas_call(factor_kernel, out_shape=(jax.ShapeDtypeStruct(residual.sh...  38.9 us
    dot_general x1, matrix products, apply_strips(): result = jnp.einsum('ikab,ikbc->iac', strips, chosen, precision=HIGHEST)  33.5 us
    all_to_all x1, blocking collectives, apply_near_field(): return lax.all_to_all(image, 'rhs', split_axis=0, concat_axis=1, tiled=True)  32.8 us
    all_to_all x1, blocking collectives, apply_near_field(): lax.all_to_all(vector_block, 'rhs', split_axis=1, concat_axis=0, tiled=True)  29.3 us
    unnamed x10, local copies, waits for them, and re-layouts  24.9 us
    gather x1, local copies, waits for them, and re-layouts, apply_strips(): chosen = pieces[positions]  24.7 us
  transfers between devices with their start and end apart: 6, of which 3 were waited for; matrix products, arithmetic and copies ran while one was open for 3% of the time, Pallas kernels for 0%

profile of v1, /device:TPU:1, one launch (start us, length us, event | category | flops | bytes accessed | tf_op | source)
XLA Modules:
  0.0 510.2 jit_solution(2496085992517580435)
XLA Ops:
  0.6 1.9 copy.12
  2.6 29.3 %all_to_all.38 = f32[256,4,512]{0,2,1:T(8,128)} all-to-all(f32[256,4,512]{0,2,1:T(8,128)S(1)} %bitcast.36), channel_id=1, replica_groups=mesh['blk'=32,'rhs'=4] {'rhs'}, dimensions={1} | all-to-all | bytes 4194304 | tf_op jit(solution)/shard_map/all_to_all | solution.py:306
  31.8 1.9 copy.13
  33.7 4.3 collective-permute-start
  38.0 1.6 collective-permute-start.1
  39.7 1.3 collective-permute-start.2
  40.9 5.9 %collective-permute-start.3 = (f32[1024,512]{1,0:T(8,128)S(1)}, f32[1024,512]{1,0:T(8,128)}, u32[]{:S(2)}, u32[]{:S(2)}) collective-permute-start(f32[1024,512]{1,0:T(8,128)S(1)} %bitcast.30), channel_id=1, source_target_pairs={{0,124},{4,0},{8,4},{12,8},{16,12},{20,16},{24,20},{28,24},{32,28}... | collective-permute-start | bytes 6291464 | tf_op jit(solution)/shard_map/ppermute | solution.py:291
  46.8 0.0 collective-permute-start.4
  46.9 41.7 %collective-permute-done = f32[1024,512]{1,0:T(8,128)S(1)} collective-permute-done((f32[1024,512]{1,0:T(8,128)S(1)}, f32[1024,512]{1,0:T(8,128)S(1)}, u32[]{:S(2)}, u32[]{:S(2)}) %collective-permute-start) | collective-permute-done | bytes 2097184 | tf_op jit(solution)/shard_map/ppermute | solution.py:291
  88.6 0.0 copy-start
  88.6 1.3 copy-done
  89.9 2.4 collective-permute-start.5
  92.3 0.7 compare_select_fusion
  93.0 0.1 reshape.36
  93.1 3.2 constant_dynamic-update-slice_fusion.6
  96.2 83.1 %collective-permute-done.1 = f32[1024,512]{1,0:T(8,128)} collective-permute-done((f32[1024,512]{1,0:T(8,128)S(1)}, f32[1024,512]{1,0:T(8,128)}, u32[]{:S(2)}, u32[]{:S(2)}) %collective-permute-start.1) | collective-permute-done | bytes 2097184 | tf_op jit(solution)/shard_map/ppermute | solution.py:291
  179.3 3.1 constant_dynamic-update-slice_fusion.5
  182.4 0.0 collective-permute-done.2
  182.4 3.1 constant_dynamic-update-slice_fusion.4
  185.4 1.5 constant_dynamic-update-slice_fusion.3
  187.0 0.0 collective-permute-done.3
  187.0 3.1 constant_dynamic-update-slice_fusion.2
  190.0 0.0 collective-permute-done.4
  190.1 3.1 constant_dynamic-update-slice_fusion.1
  193.2 48.1 %collective-permute-done.5 = f32[1024,512]{1,0:T(8,128)} collective-permute-done((f32[1024,512]{1,0:T(8,128)S(1)}, f32[1024,512]{1,0:T(8,128)}, u32[]{:S(2)}, u32[]{:S(2)}) %collective-permute-start.5) | collective-permute-done | bytes 2097184 | tf_op jit(solution)/shard_map/ppermute | solution.py:291
  241.3 3.1 constant_dynamic-update-slice_fusion
  244.4 24.7 %gather_fusion = f32[200,128,512]{2,1,0:T(8,128)} fusion(f32[56,128,512]{2,1,0:T(8,128)} %bitcast.3, s32[1024]{0:T(1024)S(1)} %pad_clamp_fusion), kind=kCustom, calls=%fused_computation | custom fusion | bytes 104858400 | tf_op jit(solution)/shard_map/gather | solution.py:298
  269.1 33.5 %fusion.1 = f32[8,512,128,1]{1,2,3,0:T(8,128)S(1)} fusion(f32[8,25,128,512]{3,2,1,0:T(8,128)} %bitcast.20, f32[8,25,128,128]{3,2,1,0:T(8,128)} %param.4), kind=kOutput, calls=%fused_computation.14 | convolution fusion | flops 20132659200 | bytes 67633152 | tf_op jit(solution)/shard_map/ikab,ikbc->iac/dot_general | solution.py:299
  302.6 32.8 %all_to_all.39 = f32[4,256,512]{2,1,0:T(8,128)S(1)} all-to-all(f32[4,256,512]{2,1,0:T(8,128)S(1)} %bitcast.26), channel_id=1, replica_groups=mesh['blk'=32,'rhs'=4] {'rhs'}, dimensions={0} | all-to-all | bytes 4194304 | tf_op jit(solution)/shard_map/all_to_all | solution.py:317
  335.4 1.5 copy.16
  337.0 14.3 %local_coeffs.1 = f32[4,16,128,128]{3,2,1,0:T(8,128)} custom-call(f32[4,256,2048]{2,1,0:T(8,128)} %basis_ref.3, f32[256,2048]{1,0:T(8,128)} %bitcast.23), custom_call_target="tpu_custom_call" | custom-call | tf_op jit(solution)/shard_map/local_coeffs/pallas_call | solution.py:182
  351.3 65.6 %all_sum_8192.1 = f32[8192,128]{1,0:T(8,128)} custom-call(f32[8192,128]{1,0:T(8,128)} %bitcast.25), custom_call_target="tpu_custom_call" | custom-call | tf_op jit(solution)/shard_map/all_sum_8192/pallas_call | solution.py:161
  416.9 16.2 %local_residual.1 = (f32[256,2048]{1,0:T(8,128)}, f32[16,128,128]{2,1,0:T(8,128)}) custom-call(f32[4,256,2048]{2,1,0:T(8,128)} %basis_ref.3, f32[256,2048]{1,0:T(8,128)} %bitcast.24, f32[4,16,128,128]{3,2,1,0:T(8,128)} %bitcast.21), custom_call_target="tpu_custom_call" | custom-call | tf_op jit(solution)/shard_map/local_residual/pallas_call | solution.py:206
  433.2 33.4 %all_sum_2048.1 = f32[2048,128]{1,0:T(8,128)} custom-call(f32[2048,128]{1,0:T(8,128)} %bitcast.38), custom_call_target="tpu_custom_call" | custom-call | tf_op jit(solution)/shard_map/all_sum_2048/pallas_call | solution.py:161
  466.6 38.9 %factor_and_solve.1 = (f32[256,2048]{1,0:T(8,128)}, f32[16,128,128]{2,1,0:T(8,128)}) custom-call(f32[16,128,128]{2,1,0:T(8,128)} %bitcast.37, f32[256,2048]{1,0:T(8,128)} %get-tuple-element.8.residual_ref), custom_call_target="tpu_custom_call" | custom-call | tf_op jit(solution)/shard_map/factor_and_solve/pallas_call | solution.py:279
  505.5 4.7 copy.24
  (1 shorter events, 0.0 us)
Async XLA Ops:
  33.7 54.8 %collective-permute-start = (f32[1024,512]{1,0:T(8,128)S(1)}, f32[1024,512]{1,0:T(8,128)S(1)}, u32[]{:S(2)}, u32[]{:S(2)}) collective-permute-start(f32[1024,512]{1,0:T(8,128)S(1)} %bitcast.27), channel_id=1, source_target_pairs={{0,12},{4,16},{8,20},{12,24},{16,28},{20,32},{24,36},{28,40},{32,4... | collective-permute-start | bytes 6291464 | tf_op jit(solution)/shard_map/ppermute | solution.py:291
  38.0 141.3 %collective-permute-start.1 = (f32[1024,512]{1,0:T(8,128)S(1)}, f32[1024,512]{1,0:T(8,128)}, u32[]{:S(2)}, u32[]{:S(2)}) collective-permute-start(f32[1024,512]{1,0:T(8,128)S(1)} %bitcast.28), channel_id=1, source_target_pairs={{0,8},{4,12},{8,16},{12,20},{16,24},{20,28},{24,32},{28,36},{32,40... | collective-permute-start | bytes 6291464 | tf_op jit(solution)/shard_map/ppermute | solution.py:291
  39.7 142.7 %collective-permute-start.2 = (f32[1024,512]{1,0:T(8,128)S(1)}, f32[1024,512]{1,0:T(8,128)}, u32[]{:S(2)}, u32[]{:S(2)}) collective-permute-start(f32[1024,512]{1,0:T(8,128)S(1)} %bitcast.29), channel_id=1, source_target_pairs={{0,4},{4,8},{8,12},{12,16},{16,20},{20,24},{24,28},{28,32},{32,36}... | collective-permute-start | bytes 6291464 | tf_op jit(solution)/shard_map/ppermute | solution.py:291
  40.9 146.0 %collective-permute-start.3 = (f32[1024,512]{1,0:T(8,128)S(1)}, f32[1024,512]{1,0:T(8,128)}, u32[]{:S(2)}, u32[]{:S(2)}) collective-permute-start(f32[1024,512]{1,0:T(8,128)S(1)} %bitcast.30), channel_id=1, source_target_pairs={{0,124},{4,0},{8,4},{12,8},{16,12},{20,16},{24,20},{28,24},{32,28}... | collective-permute-start | bytes 6291464 | tf_op jit(solution)/shard_map/ppermute | solution.py:291
  46.8 143.2 %collective-permute-start.4 = (f32[1024,512]{1,0:T(8,128)S(1)}, f32[1024,512]{1,0:T(8,128)}, u32[]{:S(2)}, u32[]{:S(2)}) collective-permute-start(f32[1024,512]{1,0:T(8,128)S(1)} %bitcast.31), channel_id=1, source_target_pairs={{0,120},{4,124},{8,0},{12,4},{16,8},{20,12},{24,16},{28,20},{32,24... | collective-permute-start | bytes 6291464 | tf_op jit(solution)/shard_map/ppermute | solution.py:291
  88.6 1.3 copy-start
  89.9 151.4 %collective-permute-start.5 = (f32[1024,512]{1,0:T(8,128)S(1)}, f32[1024,512]{1,0:T(8,128)}, u32[]{:S(2)}, u32[]{:S(2)}) collective-permute-start(f32[1024,512]{1,0:T(8,128)S(1)} %bitcast.32), channel_id=1, source_target_pairs={{0,116},{4,120},{8,124},{12,0},{16,4},{20,8},{24,12},{28,16},{32,2... | collective-permute-start | bytes 6291464 | tf_op jit(solution)/shard_map/ppermute | solution.py:291

commit v2 on v1

--- a/solution.py
+++ b/solution.py
@@ -286,35 +286,248 @@
     )(gram, residual)
 
 
-def from_behind(value, axis, by):
-    devices = lax.axis_size(axis)
-    return lax.ppermute(value, axis, [(i, (i + by) % devices) for i in range(devices)])
-
-
-def apply_strips(window, positions, strips):
-    block = strips.shape[2]
-    width = window.shape[1]
-    pieces = window.reshape(window.shape[0] // block, block, width)
-    chosen = pieces[positions]
-    result = jnp.einsum("ikab,ikbc->iac", strips, chosen, precision=HIGHEST)
-    return result.reshape(strips.shape[0] * block, width)
+SLOTS = 7
+SLOT_OFFSETS = (0, 1, -2, 2, -1, 3, -3)
+SLOT_ORIGIN = (0, 1, 0, 0, 1, 1, 1)
+CHUNKS = 4
+PIECE = 256
+BLOCK = 128
+
+
+def apply_kernel(
+    index_ref, present_ref, strips_ref, vector_ref, out_ref,
+    high_ref, low_ref, window, stage_even, stage_odd, image, strip_sem, copy_sem, recv_sem, exit_recv, own_send, relay_send, entry_send,
+    exit_send,
+):
+    blk, rhs = lax.axis_index("blk"), lax.axis_index("rhs")
+    x_lo, core = rhs // 2, rhs % 2
+    odd = blk % 2
+    sign = 1 - 2 * odd
+
+    def peer(t):
+        return (x_lo + t // 2) % 2, (core + t % 2) % 2
+
+    def quarter(at):
+        return ((at[0] + odd) % 2) * 2 + at[1]
+
+    def group_device(t):
+        x, c = peer(t)
+        return {"blk": blk, "rhs": x * 2 + c}
+
+    ahead = {"blk": (blk + 32 + 2 * sign) % 32, "rhs": rhs}
+    behind = {"blk": (blk + 32 - 2 * sign) % 32, "rhs": rhs}
+    partner = {"blk": blk + sign, "rhs": (1 - x_lo) * 2 + core}
+    columns = quarter((x_lo, core)) * (CHUNKS * GROUP)
+
+    def piece(chunk, slot, t):
+        x, c = peer(2 * SLOT_ORIGIN[slot] + t)
+        return window.at[chunk, slot, pl.ds((x * 2 + c) * PIECE, PIECE)]
+
+    def remote(src, dst, send, recv, device):
+        return pltpu.make_async_remote_copy(
+            src_ref=src, dst_ref=dst, send_sem=send, recv_sem=recv, device_id=device, device_id_type=MESH
+        )
+
+    def strip_copy(i, lane):
+        return pltpu.make_async_copy(strips_ref.at[i], (stage_even, stage_odd)[lane], strip_sem.at[lane])
+
+    def own_copy(chunk):
+        cols = pl.ds(pl.multiple_of(columns + chunk * GROUP, GROUP), GROUP)
+        return pltpu.make_async_copy(vector_ref.at[:, cols], piece(chunk, 0, 0), copy_sem.at[chunk])
+
+    def entry_copy(chunk, t):
+        cols = pl.ds(pl.multiple_of(quarter(peer(t)) * (CHUNKS * GROUP) + chunk * GROUP, GROUP), GROUP)
+        return remote(
+            vector_ref.at[:, cols], piece(chunk, 0, 0), entry_send.at[chunk, t - 1], recv_sem.at[chunk, 0, t],
+            group_device(t),
+        )
+
+    def exit_copy(chunk, t):
+        x, c = peer(t)
+        cols = pl.ds(pl.multiple_of(columns + chunk * GROUP, GROUP), GROUP)
+        return remote(
+            image.at[chunk, pl.ds((x * 2 + c) * PIECE, PIECE)], out_ref.at[:, cols], exit_send.at[chunk, t - 1],
+            exit_recv.at[chunk, t - 1], group_device(t),
+        )
+
+    def send_copy(chunk, t, way):
+        slot, device = ((1, partner), (2, ahead), (3, behind))[way]
+        x, c = peer(t)
+        dst = window.at[chunk, slot, pl.ds((x * 2 + c) * PIECE, PIECE)]
+        return remote(piece(chunk, 0, t), dst, own_send.at[chunk, t, way], recv_sem.at[chunk, slot, t], device)
+
+    def relay_copy(chunk, t, way):
+        source, slot, device = ((1, 5, behind), (3, 4, partner), (4, 6, ahead))[way]
+        x, c = peer(2 * SLOT_ORIGIN[source] + t)
+        dst = window.at[chunk, slot, pl.ds((x * 2 + c) * PIECE, PIECE)]
+        return remote(piece(chunk, source, t), dst, relay_send.at[chunk, t, way], recv_sem.at[chunk, slot, t], device)
+
+    def arrived(chunk, slot, t):
+        at = piece(chunk, slot, t)
+        remote(at, at, own_send.at[chunk, t, 0], recv_sem.at[chunk, slot, t], partner).wait_recv()
+
+    def send_own(chunk, t):
+        if t == 0:
+            own_copy(chunk).wait()
+        else:
+            arrived(chunk, 0, t)
+        for way in range(3):
+            send_copy(chunk, t, way).start()
+
+    def relay(chunk, t, way):
+        arrived(chunk, (1, 3, 4)[way], t)
+        relay_copy(chunk, t, way).start()
+
+    def build(i, lane):
+        stage = (stage_even, stage_odd)[lane]
+        strip_copy(i, lane).wait()
+        rows = slice(i * BLOCK, (i + 1) * BLOCK)
+
+        def one_slot(slot, carry):
+            for j in range(8):
+                at = slot * 8 + j
+                tile = stage[index_ref[i, at]] * present_ref[i, at]
+                high, low = split(tile)
+                high_ref[slot, rows, j * BLOCK : (j + 1) * BLOCK] = high
+                low_ref[slot, rows, j * BLOCK : (j + 1) * BLOCK] = low
+            return carry
+
+        lax.fori_loop(0, SLOTS, one_slot, 0)
+
+        if i + 2 < 8:
+            strip_copy(i + 2, lane).start()
+
+    def multiply(chunk, first, last):
+        def one(step, carry):
+            slot, k = step // 4, pl.multiple_of((step % 4) * PIECE, PIECE)
+            high, low = split(window[chunk, slot, pl.ds(k, PIECE)])
+            both = dot1(high_ref[slot, :, pl.ds(k, PIECE)], jnp.concatenate([high, low], axis=1), 1, 0)
+            rest = dot1(low_ref[slot, :, pl.ds(k, PIECE)], high, 1, 0)
+            image[chunk] = image[chunk] + (both[:, :GROUP] + (both[:, GROUP:] + rest))
+            return carry
+
+        lax.fori_loop(4 * first, 4 * last, one, 0)
+
+    def finish(chunk):
+        cols = pl.ds(pl.multiple_of(columns + chunk * GROUP, GROUP), GROUP)
+        out_ref[:, cols] = image[chunk, pl.ds(pl.multiple_of(rhs * PIECE, PIECE), PIECE)]
+        for t in (3, 2, 1):
+            exit_copy(chunk, t).start()
+
+    def tick(chunk, t, now, before, after):
+        if now and t < 3:
+            send_own(chunk, t + 1)
+        elif now and after is True:
+            send_own(chunk + 1, 0)
+        elif now:
+
+            @pl.when(after)
+            def _():
+                send_own(chunk + 1, 0)
+
+        back = chunk - 1
+        for way, lag in ((0, 1), (1, 1), (2, 2)):
+            if t >= lag and now:
+                relay(chunk, t - lag, way)
+            elif t < lag and before:
+                relay(back, t - lag + 4, way)
+        if before:
+            if t == 0:
+                for u in range(4):
+                    arrived(back, 2, u)
+                multiply(back, 1, 3)
+            if t == 1:
+                multiply(back, 3, 4)
+            if t == 2:
+                for u in range(4):
+                    arrived(back, 5, u)
+                multiply(back, 4, 6)
+            if t == 3:
+                for u in range(4):
+                    arrived(back, 6, u)
+                multiply(back, 6, 7)
+                finish(back)
+
+    for i in range(2):
+        strip_copy(i, i).start()
+    for chunk in range(CHUNKS):
+        own_copy(chunk).start()
+
+    barrier = pltpu.get_barrier_semaphore()
+    for device in [partner, ahead, behind] + [group_device(t) for t in (1, 2, 3)]:
+        pl.semaphore_signal(barrier, inc=1, device_id=device, device_id_type=MESH)
+    pl.semaphore_wait(barrier, 6)
+
+    for chunk in range(CHUNKS):
+        for t in (2, 3, 1):
+            entry_copy(chunk, t).start()
+    send_own(0, 0)
+    image[...] = jnp.zeros_like(image)
+    for t in range(4):
+        tick(0, t, True, False, True)
+        for i in (2 * t, 2 * t + 1):
+            build(i, i % 2)
+    multiply(0, 0, 1)
+
+    def body(chunk, carry):
+        for t in range(4):
+            tick(chunk, t, True, True, chunk + 1 < CHUNKS)
+        multiply(chunk, 0, 1)
+        return carry
+
+    lax.fori_loop(1, CHUNKS, body, 0)
+    for t in range(4):
+        tick(CHUNKS, t, False, True, False)
+
+    def drain(chunk, carry):
+        for t in (1, 2, 3):
+            exit_copy(chunk, t).wait_recv()
+            exit_copy(chunk, t).wait_send()
+            entry_copy(chunk, t).wait_send()
+        for t in range(4):
+            for way in range(3):
+                send_copy(chunk, t, way).wait_send()
+                relay_copy(chunk, t, way).wait_send()
+        return carry
+
+    lax.fori_loop(0, CHUNKS, drain, 0)
 
 
 def apply_near_field(strips, near_cols, vector_block):
-    local_blocks = strips.shape[0]
-    total_blocks = local_blocks * lax.axis_size("blk")
-    row_form = lax.all_to_all(vector_block, "rhs", split_axis=1, concat_axis=0, tiled=True)
-    gathered = []
-    for offset in range(-HOPS, HOPS + 1):
-        if offset == 0:
-            gathered.append(row_form)
-        else:
-            gathered.append(from_behind(row_form, "blk", -offset))
-    window = jnp.concatenate(gathered, axis=0)
-    first_block = (lax.axis_index("blk") - HOPS) * local_blocks
-    positions = jnp.mod(near_cols - first_block, total_blocks)
-    image = apply_strips(window, positions, strips)
-    return lax.all_to_all(image, "rhs", split_axis=0, concat_axis=1, tiled=True)
+    blocks, near = near_cols.shape
+    total = blocks * lax.axis_size("blk")
+    blk = lax.axis_index("blk")
+    sign = 1 - 2 * (blk % 2)
+    groups = blk + sign * jnp.array(SLOT_OFFSETS, jnp.int32)
+    target = jnp.mod(groups[:, None] * blocks + jnp.arange(blocks, dtype=jnp.int32)[None], total).reshape(-1)
+    match = near_cols[:, :, None] == target[None, None]
+    index = jnp.sum(jnp.where(match, jnp.arange(near, dtype=jnp.int32)[None, :, None], 0), axis=1)
+    present = jnp.sum(jnp.where(match, 1.0, 0.0), axis=1).astype(F32)
+    rows, width = vector_block.shape
+    smem = pl.BlockSpec(memory_space=pltpu.SMEM)
+    anywhere = pl.BlockSpec(memory_space=pl.ANY)
+    dma = pltpu.SemaphoreType.DMA
+    size = blocks * BLOCK
+    return pl.pallas_call(
+        apply_kernel,
+        out_shape=jax.ShapeDtypeStruct((rows, width), F32),
+        in_specs=[smem, smem, anywhere, anywhere],
+        out_specs=VMEM_SPEC,
+        scratch_shapes=[
+            pltpu.VMEM((SLOTS, size, size), BF16),
+            pltpu.VMEM((SLOTS, size, size), BF16),
+            pltpu.VMEM((CHUNKS, SLOTS, size, GROUP), F32),
+            pltpu.VMEM((near, BLOCK, BLOCK), F32),
+            pltpu.VMEM((near, BLOCK, BLOCK), F32),
+            pltpu.VMEM((CHUNKS, size, GROUP), F32),
+            dma((2,)), dma((CHUNKS,)), dma((CHUNKS, SLOTS, 4)), dma((CHUNKS, 3)),
+            dma((CHUNKS, 4, 3)), dma((CHUNKS, 4, 3)), dma((CHUNKS, 3)), dma((CHUNKS, 3)),
+        ],
+        compiler_params=pltpu.CompilerParams(
+            collective_id=3, has_side_effects=True, vmem_limit_bytes=64_000_000
+        ),
+        name="apply_near_field",
+    )(index, present, strips, vector_block)
 
 
 def local(strips, near_cols, vector_block, basis):

time: 512 us -> 285 us (0.56)
  waiting for transfers between devices: 173 us -> 0 us
  Pallas kernels: 169 us -> 276 us
  blocking collectives: 62.1 us -> 0 us
  local copies, waits for them, and re-layouts: 56.3 us -> 5.55 us
  matrix products: 33.5 us -> 0 us
  starting transfers between devices: 15.5 us -> 0 us
    ppermute x6 -> x0, waiting for transfers between devices: 173 us -> none  [from_behind(): lax.ppermute(value, axis, [(i, (i + by) % devices) for i in range(devices)])]
    pallas_call x0 -> x1, Pallas kernels: none -> 118 us  [apply_near_field(): pl.pallas_call(apply_kernel, out_shape=jax.ShapeDtypeStruct((rows, width)...]
    all_to_all x2 -> x0, blocking collectives: 62.1 us -> none  [the longest x1 32.8 us: apply_near_field(): return lax.all_to_all(image, 'rhs', split_axis=0, concat_axis=1, tiled=True)]
    dot_general x1 -> x0, matrix products: 33.5 us -> none  [apply_strips(): result = jnp.einsum('ikab,ikbc->iac', strips, chosen, precision=HIGHEST)]
    gather x1 -> x0, local copies, waits for them, and re-layouts: 24.7 us -> none  [apply_strips(): chosen = pieces[positions]]
    unnamed x10 -> x2, local copies, waits for them, and re-layouts: 24.9 us -> 5.47 us
    ppermute x6 -> x0, starting transfers between devices: 15.5 us -> none  [from_behind(): lax.ppermute(value, axis, [(i, (i + by) % devices) for i in range(devices)])]
    pallas_call x2, Pallas kernels: 99 us -> 87.8 us  [all_sum(): pl.pallas_call(functools.partial(all_sum_kernel, shares), out_shape=jax.S...]
  transfers between devices with their start and end apart: 6 -> 0, of which waited for: 3 -> 0; matrix products, arithmetic and copies ran while one was open for 3% -> 0% of each run, Pallas kernels for 0% -> 0%
where the time goes in v2:
time: 285 us; the launch traced here: 284 us
  Pallas kernels  276 us (97%)
  local copies, waits for them, and re-layouts  5.55 us (2%)
    pallas_call x1, Pallas kernels, apply_near_field(): pl.pallas_call(apply_kernel, out_shape=jax.ShapeDtypeStruct((rows, width)...  118 us
    pallas_call x2, Pallas kernels, all_sum(): pl.pallas_call(functools.partial(all_sum_kernel, shares), out_shape=jax.S...  87.8 us
    pallas_call x1, Pallas kernels, factor_and_solve(): pl.pallas_call(factor_kernel, out_shape=(jax.ShapeDtypeStruct(residual.sh...  38.9 us
    pallas_call x1, Pallas kernels, local_residual(): pl.pallas_call(residual_kernel, grid=(groups,), out_shape=(jax.ShapeDtype...  16.2 us
    pallas_call x1, Pallas kernels, local_coeffs(): pl.pallas_call(coeffs_kernel, grid=(groups,), out_shape=jax.ShapeDtypeStr...  14.3 us

profile of v2, /device:TPU:1, one launch (start us, length us, event | category | flops | bytes accessed | tf_op | source)
XLA Modules:
  0.0 283.9 jit_solution(4002263841887978005)
XLA Ops:
  0.6 0.7 add_multiply_fusion
  1.3 0.1 iota_add_fusion
  1.4 0.1 add.46
  1.5 0.8 copy.8
  2.2 0.7 fusion.index_ref
  2.9 0.7 fusion.1.present_ref
  3.6 118.2 %apply_near_field.1.image_ref = f32[256,2048]{1,0:T(8,128)} custom-call(s32[8,56]{1,0:T(8,128)} %fusion.index_ref, f32[8,56]{1,0:T(8,128)} %fusion.1.present_ref, f32[8,25,128,128]{3,2,1,0:T(8,128)} %strips_ref.1, f32[256,2048]{1,0:T(8,128)} %vector_ref.1), custom_call_target="tpu_custom_call" | custom-call | tf_op jit(solution)/shard_map/apply_near_field/pallas_call | solution.py:511
  121.9 14.3 %local_coeffs.1 = f32[4,16,128,128]{3,2,1,0:T(8,128)} custom-call(f32[4,256,2048]{2,1,0:T(8,128)} %basis_ref.3, f32[256,2048]{1,0:T(8,128)} %apply_near_field.1.image_ref), custom_call_target="tpu_custom_call" | custom-call | tf_op jit(solution)/shard_map/local_coeffs/pallas_call | solution.py:182
  136.2 54.0 %all_sum_8192.1 = f32[8192,128]{1,0:T(8,128)} custom-call(f32[8192,128]{1,0:T(8,128)} %bitcast.6), custom_call_target="tpu_custom_call" | custom-call | tf_op jit(solution)/shard_map/all_sum_8192/pallas_call | solution.py:161
  190.2 16.2 %local_residual.1 = (f32[256,2048]{1,0:T(8,128)}, f32[16,128,128]{2,1,0:T(8,128)}) custom-call(f32[4,256,2048]{2,1,0:T(8,128)} %basis_ref.3, f32[256,2048]{1,0:T(8,128)} %apply_near_field.1.image_ref, f32[4,16,128,128]{3,2,1,0:T(8,128)} %bitcast.4), custom_call_target="tpu_custom_call" | custom-call | tf_op jit(solution)/shard_map/local_residual/pallas_call | solution.py:206
  206.4 33.8 %all_sum_2048.1 = f32[2048,128]{1,0:T(8,128)} custom-call(f32[2048,128]{1,0:T(8,128)} %bitcast.8), custom_call_target="tpu_custom_call" | custom-call | tf_op jit(solution)/shard_map/all_sum_2048/pallas_call | solution.py:161
  240.3 38.9 %factor_and_solve.1 = (f32[256,2048]{1,0:T(8,128)}, f32[16,128,128]{2,1,0:T(8,128)}) custom-call(f32[16,128,128]{2,1,0:T(8,128)} %bitcast.7, f32[256,2048]{1,0:T(8,128)} %get-tuple-element.8.residual_ref), custom_call_target="tpu_custom_call" | custom-call | tf_op jit(solution)/shard_map/factor_and_solve/pallas_call | solution.py:279
  279.2 4.7 %copy.10 = f32[4,16,128,128]{3,2,1,0:T(8,128)} copy(f32[4,16,128,128]{3,2,1,0:T(8,128)} %bitcast.5) | data formatting | bytes 8388608
  (1 shorter events, 0.0 us)

commit v3 on v2

--- a/solution.py
+++ b/solution.py
@@ -169,55 +169,78 @@
     )(value)
 
 
+PER_STEP = 4
+
+
+def beside(high, low):
+    return jnp.concatenate([high, low], axis=1)
+
+
 def coeffs_kernel(basis_ref, image_ref, out_ref):
-    ih, il = split(image_ref[...])
-    for m in range(basis_ref.shape[0]):
-        bh, bl = split(basis_ref[m])
-        out_ref[m, 0] = dot1(bh, ih, 0, 0) + (dot1(bh, il, 0, 0) + dot1(bl, ih, 0, 0))
+    for g in range(PER_STEP):
+        columns = slice(g * GROUP, (g + 1) * GROUP)
+        ih, il = split(image_ref[:, columns])
+        bh, bl = split(jnp.concatenate([basis_ref[m, :, columns] for m in range(basis_ref.shape[0])], axis=1))
+        both = dot1(bh, beside(ih, il), 0, 0)
+        value = both[:, :GROUP] + (both[:, GROUP:] + dot1(bl, ih, 0, 0))
+        for m in range(basis_ref.shape[0]):
+            out_ref[m, g] = value[m * GROUP : (m + 1) * GROUP]
 
 
 def local_coeffs(basis, image):
     count, rows, width = basis.shape
     groups = width // GROUP
+    wide = PER_STEP * GROUP
     return pl.pallas_call(
         coeffs_kernel,
-        grid=(groups,),
+        grid=(groups // PER_STEP,),
         out_shape=jax.ShapeDtypeStruct((count, groups, GROUP, GROUP), F32),
         in_specs=[
-            pl.BlockSpec((count, rows, GROUP), lambda g: (0, 0, g)),
-            pl.BlockSpec((rows, GROUP), lambda g: (0, g)),
+            pl.BlockSpec((count, rows, wide), lambda g: (0, 0, g)),
+            pl.BlockSpec((rows, wide), lambda g: (0, g)),
         ],
-        out_specs=pl.BlockSpec((count, 1, GROUP, GROUP), lambda g: (0, g, 0, 0)),
+        out_specs=pl.BlockSpec((count, PER_STEP, GROUP, GROUP), lambda g: (0, g, 0, 0)),
         name="local_coeffs",
     )(basis, image)
 
 
-def residual_kernel(basis_ref, image_ref, coeffs_ref, residual_ref, gram_ref):
-    value = image_ref[...]
-    for m in range(basis_ref.shape[0]):
-        value = value - dot3(basis_ref[m], coeffs_ref[m, 0], 1, 0)
-    residual_ref[...] = value
-    gram_ref[0] = dot3(value, value, 0, 0)
+def residual_kernel(basis_ref, image_ref, coeffs_ref, residual_ref, gram_ref, copied_ref):
+    count = basis_ref.shape[0]
+    copied_ref[...] = coeffs_ref[...]
+    for g in range(PER_STEP):
+        columns = slice(g * GROUP, (g + 1) * GROUP)
+        bh, bl = split(jnp.concatenate([basis_ref[m, :, columns] for m in range(count)], axis=1))
+        ch, cl = split(jnp.concatenate([coeffs_ref[m, g] for m in range(count)], axis=0))
+        both = dot1(bh, beside(ch, cl), 1, 0)
+        value = image_ref[:, columns] - (both[:, :GROUP] + (both[:, GROUP:] + dot1(bl, ch, 1, 0)))
+        residual_ref[:, columns] = value
+        rh, rl = split(value)
+        square = dot1(rh, beside(rh, rl), 0, 0)
+        cross = square[:, GROUP:]
+        gram_ref[g] = square[:, :GROUP] + (cross + cross.T)
 
 
 def local_residual(basis, image, coeffs):
     count, rows, width = basis.shape
     groups = width // GROUP
+    wide = PER_STEP * GROUP
     return pl.pallas_call(
         residual_kernel,
-        grid=(groups,),
+        grid=(groups // PER_STEP,),
         out_shape=(
             jax.ShapeDtypeStruct((rows, width), F32),
             jax.ShapeDtypeStruct((groups, GROUP, GROUP), F32),
+            jax.ShapeDtypeStruct(coeffs.shape, F32),
         ),
         in_specs=[
-            pl.BlockSpec((count, rows, GROUP), lambda g: (0, 0, g)),
-            pl.BlockSpec((rows, GROUP), lambda g: (0, g)),
-            pl.BlockSpec((count, 1, GROUP, GROUP), lambda g: (0, g, 0, 0)),
+            pl.BlockSpec((count, rows, wide), lambda g: (0, 0, g)),
+            pl.BlockSpec((rows, wide), lambda g: (0, g)),
+            pl.BlockSpec((count, PER_STEP, GROUP, GROUP), lambda g: (0, g, 0, 0)),
         ],
         out_specs=(
-            pl.BlockSpec((rows, GROUP), lambda g: (0, g)),
-            pl.BlockSpec((1, GROUP, GROUP), lambda g: (g, 0, 0)),
+            pl.BlockSpec((rows, wide), lambda g: (0, g)),
+            pl.BlockSpec((PER_STEP, GROUP, GROUP), lambda g: (g, 0, 0)),
+            pl.BlockSpec((count, PER_STEP, GROUP, GROUP), lambda g: (0, g, 0, 0)),
         ),
         name="local_residual",
     )(basis, image, coeffs)
@@ -272,7 +295,10 @@
         factor_ref[g] = jnp.where(row_of >= lane_of, a_ref[g].T, 0.0)
         inverse = jnp.where(row_of >= lane_of, b_ref[g], 0.0)
         columns = slice(g * GROUP, (g + 1) * GROUP)
-        new_ref[:, columns] = dot3(residual_ref[:, columns], inverse, 1, 1)
+        nh, nl = split(inverse)
+        weights = jnp.concatenate([beside(nh, nh), beside(nl, jnp.zeros_like(nl))], axis=0)
+        both = dot1(beside(*split(residual_ref[:, columns])), weights, 1, 1)
+        new_ref[:, columns] = both[:, :GROUP] + both[:, GROUP:]
 
 
 def factor_and_solve(gram, residual):
@@ -398,15 +424,14 @@
             strip_copy(i + 2, lane).start()
 
     def multiply(chunk, first, last):
-        def one(step, carry):
-            slot, k = step // 4, pl.multiple_of((step % 4) * PIECE, PIECE)
-            high, low = split(window[chunk, slot, pl.ds(k, PIECE)])
-            both = dot1(high_ref[slot, :, pl.ds(k, PIECE)], jnp.concatenate([high, low], axis=1), 1, 0)
-            rest = dot1(low_ref[slot, :, pl.ds(k, PIECE)], high, 1, 0)
+        def one(slot, carry):
+            high, low = split(window[chunk, slot])
+            both = dot1(high_ref[slot], beside(high, low), 1, 0)
+            rest = dot1(low_ref[slot], high, 1, 0)
             image[chunk] = image[chunk] + (both[:, :GROUP] + (both[:, GROUP:] + rest))
             return carry
 
-        lax.fori_loop(4 * first, 4 * last, one, 0)
+        lax.fori_loop(first, last, one, 0)
 
     def finish(chunk):
         cols = pl.ds(pl.multiple_of(columns + chunk * GROUP, GROUP), GROUP)
@@ -535,7 +560,7 @@
     partial_coeffs = local_coeffs(basis, image)
     flat = partial_coeffs.reshape(-1, GROUP)
     coeffs = all_sum(flat, (24, 24, 16), 1).reshape(partial_coeffs.shape)
-    residual, partial_gram = local_residual(basis, image, coeffs)
+    residual, partial_gram, coeffs = local_residual(basis, image, coeffs)
     gram = all_sum(partial_gram.reshape(-1, GROUP), (8, 8), 2).reshape(partial_gram.shape)
     new_block, factor = factor_and_solve(gram, residual)
     return (new_block, coeffs, factor)

time: 285 us -> 264 us (0.926)
  Pallas kernels: 276 us -> 260 us
  local copies, waits for them, and re-layouts: 5.55 us -> 0.86 us
    pallas_call x2, Pallas kernels: 30.6 us -> 18.5 us  [the longest x1 11 us: local_residual(): pl.pallas_call(residual_kernel, grid=(groups // PER_STEP,), out_shape=(ja...]
    unnamed x2 -> x1, local copies, waits for them, and re-layouts: 5.47 us -> 0.77 us
where the time goes in v3:
time: 264 us
  Pallas kernels  260 us (98%)
    pallas_call x1, Pallas kernels, apply_near_field(): pl.pallas_call(apply_kernel, out_shape=jax.ShapeDtypeStruct((rows, width)...  116 us
    pallas_call x2, Pallas kernels, all_sum(): pl.pallas_call(functools.partial(all_sum_kernel, shares), out_shape=jax.S...  87.3 us
    pallas_call x1, Pallas kernels, factor_and_solve(): pl.pallas_call(factor_kernel, out_shape=(jax.ShapeDtypeStruct(residual.sh...  38.7 us
    pallas_call x1, Pallas kernels, local_residual(): pl.pallas_call(residual_kernel, grid=(groups // PER_STEP,), out_shape=(ja...  11 us
    pallas_call x1, Pallas kernels, local_coeffs(): pl.pallas_call(coeffs_kernel, grid=(groups // PER_STEP,), out_shape=jax.S...  7.46 us

profile of v3, /device:TPU:1, one launch (start us, length us, event | category | flops | bytes accessed | tf_op | source)
XLA Modules:
  0.0 264.0 jit_solution(2229150276515323462)
XLA Ops:
  0.6 0.7 add_multiply_fusion
  1.3 0.1 iota_add_fusion
  1.4 0.1 add.46
  1.5 0.8 copy.8
  2.2 0.7 fusion.1.present_ref
  2.9 0.7 fusion.index_ref
  3.6 115.8 %apply_near_field.1.image_ref = f32[256,2048]{1,0:T(8,128)} custom-call(s32[8,56]{1,0:T(8,128)} %fusion.index_ref, f32[8,56]{1,0:T(8,128)} %fusion.1.present_ref, f32[8,25,128,128]{3,2,1,0:T(8,128)} %strips_ref.1, f32[256,2048]{1,0:T(8,128)} %vector_ref.1), custom_call_target="tpu_custom_call" | custom-call | tf_op jit(solution)/shard_map/apply_near_field/pallas_call | solution.py:536
  119.4 7.5 %local_coeffs.1 = f32[4,16,128,128]{3,2,1,0:T(8,128)} custom-call(f32[4,256,2048]{2,1,0:T(8,128)} %basis_ref.3, f32[256,2048]{1,0:T(8,128)} %apply_near_field.1.image_ref), custom_call_target="tpu_custom_call" | custom-call | tf_op jit(solution)/shard_map/local_coeffs/pallas_call | solution.py:194
  126.9 53.7 %all_sum_8192.1 = f32[8192,128]{1,0:T(8,128)} custom-call(f32[8192,128]{1,0:T(8,128)} %bitcast.5), custom_call_target="tpu_custom_call" | custom-call | tf_op jit(solution)/shard_map/all_sum_8192/pallas_call | solution.py:161
  180.6 11.0 %local_residual.1 = (f32[256,2048]{1,0:T(8,128)}, f32[16,128,128]{2,1,0:T(8,128)}, f32[4,16,128,128]{3,2,1,0:T(8,128)}) custom-call(f32[4,256,2048]{2,1,0:T(8,128)} %basis_ref.3, f32[256,2048]{1,0:T(8,128)} %apply_near_field.1.image_ref, f32[4,16,128,128]{3,2,1,0:T(8,128)} %bitcast.4), custom_call_target="tpu_custom_call" | custom-call | tf_op jit(solution)/shard_map/local_residual/pallas_call | solution.py:227
  191.6 33.6 %all_sum_2048.1 = f32[2048,128]{1,0:T(8,128)} custom-call(f32[2048,128]{1,0:T(8,128)} %bitcast.7), custom_call_target="tpu_custom_call" | custom-call | tf_op jit(solution)/shard_map/all_sum_2048/pallas_call | solution.py:161
  225.2 38.7 %factor_and_solve.1 = (f32[256,2048]{1,0:T(8,128)}, f32[16,128,128]{2,1,0:T(8,128)}) custom-call(f32[16,128,128]{2,1,0:T(8,128)} %bitcast.6, f32[256,2048]{1,0:T(8,128)} %get-tuple-element.9.residual_ref), custom_call_target="tpu_custom_call" | custom-call | tf_op jit(solution)/shard_map/factor_and_solve/pallas_call | solution.py:305
  (1 shorter events, 0.0 us)

commit v4 on v2

--- a/solution.py
+++ b/solution.py
@@ -25,12 +25,6 @@
     return lax.dot_general(a, b, (((ca,), (cb,)), ((), ())), preferred_element_type=F32)
 
 
-def dot3(a, b, ca, cb):
-    ah, al = split(a)
-    bh, bl = split(b)
-    return dot1(ah, bh, ca, cb) + (dot1(ah, bl, ca, cb) + dot1(al, bh, ca, cb))
-
-
 ORDERS = ((0, 1, 2), (1, 2, 0), (2, 0, 1))
 
 
@@ -51,183 +45,250 @@
     return tuple(at)
 
 
-def all_sum_kernel(shares, x_ref, out_ref, from_core, *rest):
-    parts = len(shares)
-    received, acc = rest[: 3 * parts], rest[3 * parts : 5 * parts]
-    send_sem, recv_sem = rest[5 * parts :]
+COEFF_SHARES = (24, 24, 16)
+GRAM_SHARES = (8, 8)
+HALF = 8
+
+
+def beside(high, low):
+    return jnp.concatenate([high, low], axis=1)
+
+
+def orthogonalize_kernel(
+    basis_ref, image_ref, coeffs_ref, residual_ref, gram_ref, basis_in, image_in, coeffs_part, gram_part, *rest
+):
+    coeff_count, gram_count = len(COEFF_SHARES), len(GRAM_SHARES)
+    rest = list(rest)
+
+    def take(count):
+        taken = rest[:count]
+        del rest[:count]
+        return taken
+
+    buffers = {}
+    for key, count in (("coeffs", coeff_count), ("gram", gram_count)):
+        buffers[key] = (take(1)[0], take(3 * count), take(2 * count))
+    load_sem, send_sem, recv_sem = rest
+    count = basis_ref.shape[0]
+    depth = count * GROUP
     place, core = coordinates()
-    half = x_ref.shape[0] // 2
     partner = device_of(place, 1 - core)
     peers = [device_of(moved(place, axis, by), core) for axis in range(3) for by in (1, 2, 3)]
+    own_first, other_first = core * HALF, (1 - core) * HALF
+
+    def loads(g):
+        columns = pl.ds(pl.multiple_of(g * GROUP, GROUP), GROUP)
+        return (
+            pltpu.make_async_copy(basis_ref.at[:, :, columns], basis_in.at[g], load_sem.at[0, g]),
+            pltpu.make_async_copy(image_ref.at[:, columns], image_in.at[g], load_sem.at[1, g]),
+        )
+
+    def start_loads(i, first):
+        for load in loads(first + i):
+            load.start()
+        return first
+
+    lax.fori_loop(0, HALF, start_loads, other_first)
+    lax.fori_loop(0, HALF, start_loads, own_first)
 
     barrier = pltpu.get_barrier_semaphore()
     for peer in [partner] + peers:
         pl.semaphore_signal(barrier, inc=1, device_id=peer, device_id_type=MESH)
-    pl.semaphore_wait(barrier, 10)
-
-    counter = [0]
+
+    pending = []
 
     def copy(src, dst, device):
-        at = counter[0]
-        counter[0] += 1
+        at = len(pending)
         made = pltpu.make_async_remote_copy(
             src_ref=src, dst_ref=dst, send_sem=send_sem.at[at], recv_sem=recv_sem.at[at],
             device_id=device, device_id_type=MESH,
         )
         made.start()
+        pending.append(made)
         return made
 
-    offsets, total = [], 0
-    for share in shares:
-        offsets.append(total)
-        total += 64 * share
-    mine, other = core * half, (1 - core) * half
-
-    first = [
-        copy(x_ref.at[pl.ds(other + offset, 64 * share)], from_core.at[pl.ds(offset, 64 * share)], partner)
-        for offset, share in zip(offsets, shares)
-    ]
-    pending = []
-    for part, (offset, share) in enumerate(zip(offsets, shares)):
-        first[part].wait_recv()
-        rows = pl.ds(offset, 64 * share)
-        from_core[rows] = from_core[rows] + x_ref[pl.ds(mine + offset, 64 * share)]
-
-    sources = [from_core.at[pl.ds(offset, 64 * share)] for offset, share in zip(offsets, shares)]
-    for stage in range(3):
-        copies = []
-        for part, share in enumerate(shares):
-            axis = ORDERS[part][stage]
-            size = share * 4 ** (2 - stage)
-            block = []
-            for by in (1, 2, 3):
-                to = (place[axis] + by) % 4
-                block.append(copy(
-                    sources[part].at[pl.ds(to * size, size)],
-                    received[3 * part + stage].at[by - 1],
-                    device_of(moved(place, axis, by), core),
-                ))
-            copies.append(block)
-        for part, share in enumerate(shares):
-            axis = ORDERS[part][stage]
-            size = share * 4 ** (2 - stage)
-            for made in copies[part]:
-                made.wait_recv()
-            got = received[3 * part + stage]
-            value = sources[part][pl.ds(place[axis] * size, size)] + got[0] + got[1] + got[2]
-            if stage < 2:
-                acc[2 * part + stage][...] = value
-                sources[part] = acc[2 * part + stage]
-            else:
-                sources[part] = value
-        pending += [made for block in copies for made in block]
-
-    starts = []
-    for part, share in enumerate(shares):
-        at = mine + offsets[part]
-        for stage in range(3):
-            at = at + place[ORDERS[part][stage]] * share * 4 ** (2 - stage)
-        starts.append(at)
-        out_ref[pl.ds(at, share)] = sources[part]
-    for stage in (2, 1, 0):
-        copies = []
-        for part, share in enumerate(shares):
-            axis = ORDERS[part][stage]
-            size = share * 4 ** (2 - stage)
-            at = mine + offsets[part]
-            for before in range(stage + 1):
-                at = at + place[ORDERS[part][before]] * share * 4 ** (2 - before)
-            rows = out_ref.at[pl.ds(at, size)]
-            for by in (1, 2, 3):
-                copies.append(copy(rows, rows, device_of(moved(place, axis, by), core)))
+    def basis_halves(g):
+        return split(jnp.concatenate([basis_in[g, m] for m in range(count)], axis=1))
+
+    def local_coeffs(i, first):
+        g = first + i
+        for load in loads(g):
+            load.wait()
+        ih, il = split(image_in[g])
+        bh, bl = basis_halves(g)
+        both = dot1(bh, beside(ih, il), 0, 0)
+        value = both[:, :GROUP] + (both[:, GROUP:] + dot1(bl, ih, 0, 0))
+        coeffs_part[pl.ds(pl.multiple_of(g * depth, depth), depth)] = value
+        return first
+
+    def local_residual(i, first):
+        g = first + i
+        bh, bl = basis_halves(g)
+        ch, cl = split(coeffs_ref[pl.ds(pl.multiple_of(g * depth, depth), depth)])
+        both = dot1(bh, beside(ch, cl), 1, 0)
+        value = image_in[g] - (both[:, :GROUP] + (both[:, GROUP:] + dot1(bl, ch, 1, 0)))
+        residual_ref[:, pl.ds(pl.multiple_of(g * GROUP, GROUP), GROUP)] = value
+        rh, rl = split(value)
+        square = dot1(rh, beside(rh, rl), 0, 0)
+        cross = square[:, GROUP:]
+        gram_part[pl.ds(pl.multiple_of(g * GROUP, GROUP), GROUP)] = square[:, :GROUP] + (cross + cross.T)
+        return first
+
+    def bounds(shares):
+        ends = [0]
+        for share in shares:
+            ends.append(ends[-1] + 64 * share)
+        return ends
+
+    def swap(key, shares, part_ref, part):
+        ends = bounds(shares)
+        size = ends[part + 1] - ends[part]
+        start = (1 - core) * ends[-1] + ends[part]
+        return copy(part_ref.at[pl.ds(start, size)], buffers[key][0].at[pl.ds(ends[part], size)], partner)
+
+    def scatter(key, shares, source, part, stage):
+        axis = ORDERS[part][stage]
+        size = shares[part] * 4 ** (2 - stage)
+        got = buffers[key][1][3 * part + stage]
+        return [
+            copy(
+                source.at[pl.ds((place[axis] + by) % 4 * size, size)], got.at[by - 1],
+                device_of(moved(place, axis, by), core),
+            )
+            for by in (1, 2, 3)
+        ]
+
+    def begin(key, shares, part_ref, part, swapped):
+        ends = bounds(shares)
+        size = ends[part + 1] - ends[part]
+        mine = core * ends[-1] + ends[part]
+        swapped.wait_recv()
+        from_core = buffers[key][0]
+        rows = pl.ds(ends[part], size)
+        from_core[rows] = from_core[rows] + part_ref[pl.ds(mine, size)]
+        source = from_core.at[rows]
+        return source, scatter(key, shares, source, part, 0)
+
+    def offset(shares, part, stages):
+        ends = bounds(shares)
+        at = core * ends[-1] + ends[part]
+        for stage in range(stages):
+            at = at + place[ORDERS[part][stage]] * (shares[part] * 4 ** (2 - stage))
+        return at
+
+    def gather(shares, out_ref, part, stage):
+        axis = ORDERS[part][stage]
+        size = shares[part] * 4 ** (2 - stage)
+        rows = out_ref.at[pl.ds(offset(shares, part, stage + 1), size)]
+        return [copy(rows, rows, device_of(moved(place, axis, by), core)) for by in (1, 2, 3)]
+
+    def arrive(copies):
         for made in copies:
             made.wait_recv()
-        pending += copies
-    rows = out_ref.at[pl.ds(mine, half)]
-    last = copy(rows, rows, partner)
-    last.wait_recv()
-    for made in first + pending + [last]:
+
+    def sum_up(key, shares, begun, out_ref):
+        live = dict(enumerate(begun))
+        for stage in range(3):
+            for part, share in enumerate(shares):
+                source, copies = live[part]
+                arrive(copies)
+                axis = ORDERS[part][stage]
+                size = share * 4 ** (2 - stage)
+                got = buffers[key][1][3 * part + stage]
+                value = source[pl.ds(place[axis] * size, size)] + got[0] + got[1] + got[2]
+                if stage < 2:
+                    acc = buffers[key][2][2 * part + stage]
+                    acc[...] = value
+                    live[part] = (acc, scatter(key, shares, acc, part, stage + 1))
+                else:
+                    out_ref[pl.ds(offset(shares, part, 3), share)] = value
+                    live[part] = gather(shares, out_ref, part, 2)
+        for stage in (2, 1, 0):
+            for part in range(len(shares)):
+                arrive(live[part])
+                if stage:
+                    live[part] = gather(shares, out_ref, part, stage - 1)
+                else:
+                    yield part
+
+    def give(shares, out_ref, part):
+        ends = bounds(shares)
+        rows = out_ref.at[pl.ds(core * ends[-1] + ends[part], ends[part + 1] - ends[part])]
+        return copy(rows, rows, partner)
+
+    spans = [(end // depth, last // depth) for end, last in zip(bounds(COEFF_SHARES), bounds(COEFF_SHARES)[1:])]
+    swapped = []
+    for part, (low, high) in enumerate(spans):
+        lax.fori_loop(low, high, local_coeffs, other_first)
+        if part == 0:
+            pl.semaphore_wait(barrier, 10)
+        swapped.append(swap("coeffs", COEFF_SHARES, coeffs_part, part))
+    begun = []
+    for part, (low, high) in enumerate(spans):
+        lax.fori_loop(low, high, local_coeffs, own_first)
+        begun.append(begin("coeffs", COEFF_SHARES, coeffs_part, part, swapped[part]))
+    given = []
+    for part in sum_up("coeffs", COEFF_SHARES, begun, coeffs_ref):
+        given.append(give(COEFF_SHARES, coeffs_ref, part))
+        lax.fori_loop(*spans[part], local_residual, own_first)
+
+    swapped = []
+    for part, (low, high) in enumerate(spans):
+        given[part].wait_recv()
+        lax.fori_loop(low, high, local_residual, other_first)
+        if part:
+            swapped.append(swap("gram", GRAM_SHARES, gram_part, part - 1))
+    begun = [begin("gram", GRAM_SHARES, gram_part, part, swapped[part]) for part in range(gram_count)]
+    given = [give(GRAM_SHARES, gram_ref, part) for part in sum_up("gram", GRAM_SHARES, begun, gram_ref)]
+    arrive(given)
+    for made in pending:
         made.wait_send()
 
 
-def all_sum(value, shares, collective_id):
-    rows = value.shape[0]
-    scratch = [pltpu.VMEM((rows // 2, 128), F32)]
-    for share in shares:
-        scratch += [pltpu.VMEM((3, share * 4 ** (2 - stage), 128), F32) for stage in range(3)]
-    for share in shares:
-        scratch += [pltpu.VMEM((share * 4 ** (2 - stage), 128), F32) for stage in range(2)]
-    copies = 2 * 9 * len(shares) + len(shares) + 1
-    return pl.pallas_call(
-        functools.partial(all_sum_kernel, shares),
-        out_shape=jax.ShapeDtypeStruct(value.shape, F32),
-        in_specs=[VMEM_SPEC],
-        out_specs=VMEM_SPEC,
-        scratch_shapes=scratch + [pltpu.SemaphoreType.DMA((copies,)), pltpu.SemaphoreType.DMA((copies,))],
-        compiler_params=pltpu.CompilerParams(collective_id=collective_id, has_side_effects=True),
-        name=f"all_sum_{rows}",
-    )(value)
-
-
-def coeffs_kernel(basis_ref, image_ref, out_ref):
-    ih, il = split(image_ref[...])
-    for m in range(basis_ref.shape[0]):
-        bh, bl = split(basis_ref[m])
-        out_ref[m, 0] = dot1(bh, ih, 0, 0) + (dot1(bh, il, 0, 0) + dot1(bl, ih, 0, 0))
-
-
-def local_coeffs(basis, image):
+def orthogonalize(basis, image):
     count, rows, width = basis.shape
     groups = width // GROUP
+    scratch = [
+        pltpu.VMEM((groups, count, rows, GROUP), F32),
+        pltpu.VMEM((groups, rows, GROUP), F32),
+        pltpu.VMEM((groups * count * GROUP, GROUP), F32),
+        pltpu.VMEM((groups * GROUP, GROUP), F32),
+    ]
+    copies = 0
+    for shares in (COEFF_SHARES, GRAM_SHARES):
+        scratch.append(pltpu.VMEM((64 * sum(shares), GROUP), F32))
+        for share in shares:
+            scratch += [pltpu.VMEM((3, share * 4 ** (2 - stage), GROUP), F32) for stage in range(3)]
+        for share in shares:
+            scratch += [pltpu.VMEM((share * 4 ** (2 - stage), GROUP), F32) for stage in range(2)]
+        copies += 20 * len(shares)
+    dma = pltpu.SemaphoreType.DMA
+    anywhere = pl.BlockSpec(memory_space=pl.ANY)
     return pl.pallas_call(
-        coeffs_kernel,
-        grid=(groups,),
-        out_shape=jax.ShapeDtypeStruct((count, groups, GROUP, GROUP), F32),
-        in_specs=[
-            pl.BlockSpec((count, rows, GROUP), lambda g: (0, 0, g)),
-            pl.BlockSpec((rows, GROUP), lambda g: (0, g)),
-        ],
-        out_specs=pl.BlockSpec((count, 1, GROUP, GROUP), lambda g: (0, g, 0, 0)),
-        name="local_coeffs",
+        orthogonalize_kernel,
+        out_shape=(
+            jax.ShapeDtypeStruct((groups * count * GROUP, GROUP), F32),
+            jax.ShapeDtypeStruct((rows, width), F32),
+            jax.ShapeDtypeStruct((groups * GROUP, GROUP), F32),
+        ),
+        in_specs=[anywhere, anywhere],
+        out_specs=(VMEM_SPEC, VMEM_SPEC, VMEM_SPEC),
+        scratch_shapes=scratch + [dma((2, groups)), dma((copies,)), dma((copies,))],
+        compiler_params=pltpu.CompilerParams(
+            collective_id=1, has_side_effects=True, vmem_limit_bytes=60_000_000
+        ),
+        name="orthogonalize",
     )(basis, image)
 
 
-def residual_kernel(basis_ref, image_ref, coeffs_ref, residual_ref, gram_ref):
-    value = image_ref[...]
-    for m in range(basis_ref.shape[0]):
-        value = value - dot3(basis_ref[m], coeffs_ref[m, 0], 1, 0)
-    residual_ref[...] = value
-    gram_ref[0] = dot3(value, value, 0, 0)
-
-
-def local_residual(basis, image, coeffs):
-    count, rows, width = basis.shape
-    groups = width // GROUP
-    return pl.pallas_call(
-        residual_kernel,
-        grid=(groups,),
-        out_shape=(
-            jax.ShapeDtypeStruct((rows, width), F32),
-            jax.ShapeDtypeStruct((groups, GROUP, GROUP), F32),
-        ),
-        in_specs=[
-            pl.BlockSpec((count, rows, GROUP), lambda g: (0, 0, g)),
-            pl.BlockSpec((rows, GROUP), lambda g: (0, g)),
-            pl.BlockSpec((count, 1, GROUP, GROUP), lambda g: (0, g, 0, 0)),
-        ],
-        out_specs=(
-            pl.BlockSpec((rows, GROUP), lambda g: (0, g)),
-            pl.BlockSpec((1, GROUP, GROUP), lambda g: (g, 0, 0)),
-        ),
-        name="local_residual",
-    )(basis, image, coeffs)
-
-
 STEP = 32
 
 
-def factor_kernel(gram_ref, residual_ref, new_ref, factor_ref, a_ref, b_ref):
+def factor_kernel(gram_ref, residual_ref, flat_ref, new_ref, factor_ref, coeffs_ref, a_ref, b_ref, held, in_sem, out_sem):
     groups = gram_ref.shape[0]
+    count = coeffs_ref.shape[0]
+    fetch = pltpu.make_async_copy(flat_ref, held, in_sem)
+    fetch.start()
     a_ref[...] = gram_ref[...]
     shape = (GROUP, GROUP)
     row_of = lax.broadcasted_iota(jnp.int32, shape, 0)
@@ -236,7 +297,14 @@
     b_ref[...] = jnp.broadcast_to(eye[None], (groups,) + shape)
     lane = lax.broadcasted_iota(jnp.int32, (1, 8, GROUP), 2)
     sub = lax.broadcasted_iota(jnp.int32, (1, 8, GROUP), 1)
+    stores = [
+        pltpu.make_async_copy(held.at[g], coeffs_ref.at[:, g], out_sem.at[g]) for g in range(groups)
+    ]
     for block in range(GROUP // STEP):
+        if block == 1:
+            fetch.wait()
+            for store in stores:
+                store.start()
         s = block * STEP
         o = (s + 64) % GROUP
         tiles = []
@@ -272,18 +340,33 @@
         factor_ref[g] = jnp.where(row_of >= lane_of, a_ref[g].T, 0.0)
         inverse = jnp.where(row_of >= lane_of, b_ref[g], 0.0)
         columns = slice(g * GROUP, (g + 1) * GROUP)
-        new_ref[:, columns] = dot3(residual_ref[:, columns], inverse, 1, 1)
-
-
-def factor_and_solve(gram, residual):
+        nh, nl = split(inverse)
+        weights = jnp.concatenate([beside(nh, nh), beside(nl, jnp.zeros_like(nl))], axis=0)
+        both = dot1(beside(*split(residual_ref[:, columns])), weights, 1, 1)
+        new_ref[:, columns] = both[:, :GROUP] + both[:, GROUP:]
+    for store in stores:
+        store.wait()
+
+
+def factor_and_solve(gram, residual, flat_coeffs, count):
+    groups = gram.shape[0]
+    anywhere = pl.BlockSpec(memory_space=pl.ANY)
+    shape = (groups, count, GROUP, GROUP)
     return pl.pallas_call(
         factor_kernel,
-        out_shape=(jax.ShapeDtypeStruct(residual.shape, F32), jax.ShapeDtypeStruct(gram.shape, F32)),
-        in_specs=[VMEM_SPEC, VMEM_SPEC],
-        out_specs=(VMEM_SPEC, VMEM_SPEC),
-        scratch_shapes=[pltpu.VMEM(gram.shape, F32), pltpu.VMEM(gram.shape, F32)],
+        out_shape=(
+            jax.ShapeDtypeStruct(residual.shape, F32),
+            jax.ShapeDtypeStruct(gram.shape, F32),
+            jax.ShapeDtypeStruct((count, groups, GROUP, GROUP), F32),
+        ),
+        in_specs=[VMEM_SPEC, VMEM_SPEC, anywhere],
+        out_specs=(VMEM_SPEC, VMEM_SPEC, anywhere),
+        scratch_shapes=[
+            pltpu.VMEM(gram.shape, F32), pltpu.VMEM(gram.shape, F32), pltpu.VMEM(shape, F32),
+            pltpu.SemaphoreType.DMA(()), pltpu.SemaphoreType.DMA((groups,)),
+        ],
         name="factor_and_solve",
-    )(gram, residual)
+    )(gram, residual, flat_coeffs.reshape(shape))
 
 
 SLOTS = 7
@@ -398,15 +481,14 @@
             strip_copy(i + 2, lane).start()
 
     def multiply(chunk, first, last):
-        def one(step, carry):
-            slot, k = step // 4, pl.multiple_of((step % 4) * PIECE, PIECE)
-            high, low = split(window[chunk, slot, pl.ds(k, PIECE)])
-            both = dot1(high_ref[slot, :, pl.ds(k, PIECE)], jnp.concatenate([high, low], axis=1), 1, 0)
-            rest = dot1(low_ref[slot, :, pl.ds(k, PIECE)], high, 1, 0)
+        def one(slot, carry):
+            high, low = split(window[chunk, slot])
+            both = dot1(high_ref[slot], beside(high, low), 1, 0)
+            rest = dot1(low_ref[slot], high, 1, 0)
             image[chunk] = image[chunk] + (both[:, :GROUP] + (both[:, GROUP:] + rest))
             return carry
 
-        lax.fori_loop(4 * first, 4 * last, one, 0)
+        lax.fori_loop(first, last, one, 0)
 
     def finish(chunk):
         cols = pl.ds(pl.multiple_of(columns + chunk * GROUP, GROUP), GROUP)
@@ -414,38 +496,31 @@
         for t in (3, 2, 1):
             exit_copy(chunk, t).start()
 
-    def tick(chunk, t, now, before, after):
-        if now and t < 3:
-            send_own(chunk, t + 1)
-        elif now and after is True:
-            send_own(chunk + 1, 0)
-        elif now:
-
-            @pl.when(after)
-            def _():
-                send_own(chunk + 1, 0)
-
+    def tick(chunk, t, first):
+        now = True if first else chunk < CHUNKS
         back = chunk - 1
+
+        def when(condition, action):
+            if condition is True:
+                action()
+            else:
+                pl.when(condition)(action)
+
+        if t < 3:
+            when(now, lambda: send_own(chunk, t + 1))
+        else:
+            when(True if first else chunk + 1 < CHUNKS, lambda: send_own(chunk + 1, 0))
         for way, lag in ((0, 1), (1, 1), (2, 2)):
-            if t >= lag and now:
-                relay(chunk, t - lag, way)
-            elif t < lag and before:
+            if t >= lag:
+                when(now, functools.partial(relay, chunk, t - lag, way))
+            elif not first:
                 relay(back, t - lag + 4, way)
-        if before:
-            if t == 0:
+        if not first:
+            for slot in ((2,), (), (5,), (6,))[t]:
                 for u in range(4):
-                    arrived(back, 2, u)
-                multiply(back, 1, 3)
-            if t == 1:
-                multiply(back, 3, 4)
-            if t == 2:
-                for u in range(4):
-                    arrived(back, 5, u)
-                multiply(back, 4, 6)
+                    arrived(back, slot, u)
+            multiply(back, (1, 3, 4, 6)[t], (3, 4, 6, 7)[t])
             if t == 3:
-                for u in range(4):
-                    arrived(back, 6, u)
-                multiply(back, 6, 7)
                 finish(back)
 
     for i in range(2):
@@ -464,20 +539,22 @@
     send_own(0, 0)
     image[...] = jnp.zeros_like(image)
     for t in range(4):
-        tick(0, t, True, False, True)
+        tick(0, t, True)
         for i in (2 * t, 2 * t + 1):
             build(i, i % 2)
     multiply(0, 0, 1)
 
     def body(chunk, carry):
         for t in range(4):
-            tick(chunk, t, True, True, chunk + 1 < CHUNKS)
-        multiply(chunk, 0, 1)
+            tick(chunk, t, False)
+
+        @pl.when(chunk < CHUNKS)
+        def _():
+            multiply(chunk, 0, 1)
+
         return carry
 
-    lax.fori_loop(1, CHUNKS, body, 0)
-    for t in range(4):
-        tick(CHUNKS, t, False, True, False)
+    lax.fori_loop(1, CHUNKS + 1, body, 0)
 
     def drain(chunk, carry):
         for t in (1, 2, 3):
@@ -532,12 +609,9 @@
 
 def local(strips, near_cols, vector_block, basis):
     image = apply_near_field(strips, near_cols, vector_block)
-    partial_coeffs = local_coeffs(basis, image)
-    flat = partial_coeffs.reshape(-1, GROUP)
-    coeffs = all_sum(flat, (24, 24, 16), 1).reshape(partial_coeffs.shape)
-    residual, partial_gram = local_residual(basis, image, coeffs)
-    gram = all_sum(partial_gram.reshape(-1, GROUP), (8, 8), 2).reshape(partial_gram.shape)
-    new_block, factor = factor_and_solve(gram, residual)
+    flat_coeffs, residual, gram = orthogonalize(basis, image)
+    gram = gram.reshape(-1, GROUP, GROUP)
+    new_block, factor, coeffs = factor_and_solve(gram, residual, flat_coeffs, basis.shape[0])
     return (new_block, coeffs, factor)
 
 

time: 285 us -> 247 us (0.87)
  Pallas kernels: 276 us -> 243 us
  local copies, waits for them, and re-layouts: 5.55 us -> 0.86 us
    pallas_call x4 -> x1, Pallas kernels: 118 us -> 86.6 us  [orthogonalize(): pl.pallas_call(orthogonalize_kernel, out_shape=(jax.ShapeDtypeStruct((gro...]
    unnamed x2 -> x1, local copies, waits for them, and re-layouts: 5.47 us -> 0.77 us
where the time goes in v4:
time: 247 us
  Pallas kernels  243 us (98%)
    pallas_call x1, Pallas kernels, apply_near_field(): pl.pallas_call(apply_kernel, out_shape=jax.ShapeDtypeStruct((rows, width)...  116 us
    pallas_call x1, Pallas kernels, orthogonalize(): pl.pallas_call(orthogonalize_kernel, out_shape=(jax.ShapeDtypeStruct((gro...  86.6 us
    pallas_call x1, Pallas kernels, factor_and_solve(): pl.pallas_call(factor_kernel, out_shape=(jax.ShapeDtypeStruct(residual.sh...  40.9 us

profile of v4, /device:TPU:1, one launch (start us, length us, event | category | flops | bytes accessed | tf_op | source)
XLA Modules:
  0.0 247.0 jit_solution(2064328912428141280)
XLA Ops:
  0.6 0.7 add_multiply_fusion
  1.3 0.1 iota_add_fusion
  1.4 0.1 add.46
  1.5 0.8 copy.8
  2.2 0.7 fusion.1.present_ref
  2.9 0.7 fusion.index_ref
  3.6 115.8 %apply_near_field.1.image_ref = f32[256,2048]{1,0:T(8,128)} custom-call(s32[8,56]{1,0:T(8,128)} %fusion.index_ref, f32[8,56]{1,0:T(8,128)} %fusion.1.present_ref, f32[8,25,128,128]{3,2,1,0:T(8,128)} %strips_ref.1, f32[256,2048]{1,0:T(8,128)} %vector_ref.1), custom_call_target="tpu_custom_call" | custom-call | tf_op jit(solution)/shard_map/apply_near_field/pallas_call | solution.py:588
  119.4 86.6 %orthogonalize.1 = (f32[8192,128]{1,0:T(8,128)}, f32[256,2048]{1,0:T(8,128)}, f32[2048,128]{1,0:T(8,128)}) custom-call(f32[4,256,2048]{2,1,0:T(8,128)} %basis_ref.1, f32[256,2048]{1,0:T(8,128)} %apply_near_field.1.image_ref), custom_call_target="tpu_custom_call" | custom-call | tf_op jit(solution)/shard_map/orthogonalize/pallas_call | solution.py:267
  206.0 40.9 %factor_and_solve.1 = (f32[256,2048]{1,0:T(8,128)}, f32[16,128,128]{2,1,0:T(8,128)}, f32[4,16,128,128]{3,2,1,0:T(8,128)}) custom-call(f32[16,128,128]{2,1,0:T(8,128)} %bitcast.3, f32[256,2048]{1,0:T(8,128)} %get-tuple-element.10.residual_ref, f32[16,4,128,128]{3,2,1,0:T(8,128)} %bitcast.2), custom_call_target="tpu_custom_call" | custom-call | tf_op jit(solution)/shard_map/factor_and_solve/pallas_call | solution.py:355
  (1 shorter events, 0.0 us)

commit v5 on v4

--- a/solution.py
+++ b/solution.py
@@ -10,7 +10,6 @@
 HOPS = 3
 GROUP = 128
 MESH = pl.DeviceIdType.MESH
-HIGHEST = lax.Precision.HIGHEST
 BF16, F32 = jnp.bfloat16, jnp.float32
 VMEM_SPEC = pl.BlockSpec(memory_space=pltpu.VMEM)
 
@@ -282,24 +281,26 @@
 
 
 STEP = 32
-
-
-def factor_kernel(gram_ref, residual_ref, flat_ref, new_ref, factor_ref, coeffs_ref, a_ref, b_ref, held, in_sem, out_sem):
+PIVOTS = 2
+
+
+def factor_kernel(gram_ref, residual_ref, flat_ref, new_ref, factor_ref, coeffs_ref, work_ref, held, in_sem, out_sem):
     groups = gram_ref.shape[0]
-    count = coeffs_ref.shape[0]
     fetch = pltpu.make_async_copy(flat_ref, held, in_sem)
     fetch.start()
-    a_ref[...] = gram_ref[...]
     shape = (GROUP, GROUP)
     row_of = lax.broadcasted_iota(jnp.int32, shape, 0)
     lane_of = lax.broadcasted_iota(jnp.int32, shape, 1)
     eye = jnp.where(row_of == lane_of, 1.0, 0.0).astype(F32)
-    b_ref[...] = jnp.broadcast_to(eye[None], (groups,) + shape)
-    lane = lax.broadcasted_iota(jnp.int32, (1, 8, GROUP), 2)
-    sub = lax.broadcasted_iota(jnp.int32, (1, 8, GROUP), 1)
+    for g in range(groups):
+        work_ref[g, :, :GROUP] = gram_ref[g]
+        work_ref[g, :, GROUP:] = eye
+    lane = lax.broadcasted_iota(jnp.int32, (8, GROUP), 1)
+    sub = lax.broadcasted_iota(jnp.int32, (8, GROUP), 0)
     stores = [
         pltpu.make_async_copy(held.at[g], coeffs_ref.at[:, g], out_sem.at[g]) for g in range(groups)
     ]
+    count = STEP // 8
     for block in range(GROUP // STEP):
         if block == 1:
             fetch.wait()
@@ -307,38 +308,53 @@
                 store.start()
         s = block * STEP
         o = (s + 64) % GROUP
-        tiles = []
-        for t in range(STEP // 8):
-            rows = a_ref[:, s + 8 * t : s + 8 * t + 8, :]
-            ones = jnp.where(lane == o + 8 * t + sub, 1.0, 0.0).astype(F32)
-            tiles.append(jnp.where((lane >= s) & (lane < s + STEP), rows, ones))
-        for j in range(STEP):
-            at, within = j // 8, j % 8
-            row = tiles[at][:, within : within + 1, :]
-            scaled = row / tiles[at][:, within : within + 1, s + j : s + j + 1]
-            for t in range(at, STEP // 8):
-                column = tiles[t][:, :, s + j : s + j + 1]
-                if t == at:
-                    column = jnp.where(sub > within, column, 0.0)
-                tiles[t] = tiles[t] - column * scaled
-        for t in range(STEP // 8):
-            diagonal = jnp.sum(jnp.where(lane == s + 8 * t + sub, tiles[t], 0.0), axis=2, keepdims=True)
-            tiles[t] = tiles[t] * (1.0 / jnp.sqrt(diagonal))
-        panel = jnp.concatenate(tiles, axis=1)
-        for g in range(groups):
-            inverse = panel[g, :, o : o + STEP]
-            wa = jnp.dot(inverse, a_ref[g, s : s + STEP, :], precision=HIGHEST, preferred_element_type=F32)
-            wb = jnp.dot(inverse, b_ref[g, s : s + STEP, :], precision=HIGHEST, preferred_element_type=F32)
-            a_ref[g, s : s + STEP, :] = wa
-            b_ref[g, s : s + STEP, :] = wb
+        ones = [jnp.where(lane == o + 8 * t + sub, 1.0, 0.0).astype(F32) for t in range(count)]
+        inside = (lane >= s) & (lane < s + STEP)
+        panels = [
+            [jnp.where(inside, work_ref[g, s + 8 * t : s + 8 * t + 8, :GROUP], ones[t]) for t in range(count)]
+            for g in range(groups)
+        ]
+        for first in range(0, STEP, PIVOTS):
+            at, within = first // 8, first % 8
+            for tiles in panels:
+                columns = {
+                    t: [
+                        jnp.broadcast_to(tiles[t][:, s + first + q : s + first + q + 1], (8, GROUP))
+                        for q in range(PIVOTS)
+                    ]
+                    for t in range(at, count)
+                }
+                for q in range(PIVOTS):
+                    pivot = slice(within + q, within + q + 1)
+                    inverse = 1.0 / columns[at][q][pivot]
+                    scaled = tiles[at][pivot] * inverse
+                    later = [columns[at][p][pivot] * inverse for p in range(q + 1, PIVOTS)]
+                    for t in range(at, count):
+                        column = columns[t][q]
+                        if t == at:
+                            column = jnp.where(sub > within + q, column, 0.0)
+                        tiles[t] = tiles[t] - column * scaled
+                        for p, value in zip(range(q + 1, PIVOTS), later):
+                            columns[t][p] = columns[t][p] - column * value
+        for g, tiles in enumerate(panels):
+            for t in range(count):
+                diagonal = jnp.sum(jnp.where(lane == s + 8 * t + sub, tiles[t], 0.0), axis=1, keepdims=True)
+                tiles[t] = tiles[t] * (1.0 / jnp.sqrt(diagonal))
+            inverse = jnp.concatenate(tiles, axis=0)[:, o : o + STEP]
+            high = inverse.astype(BF16).astype(F32)
+            left = jnp.concatenate([high, inverse - high, high], axis=1).astype(BF16)
+            wh, wl = split(work_ref[g, s : s + STEP])
+            rows = dot1(left, jnp.concatenate([wh, wh, wl], axis=0), 1, 0)
+            work_ref[g, s : s + STEP] = rows
             if s + STEP < GROUP:
+                rh, rl = split(rows)
+                ah, al = rh[:, :GROUP], rl[:, :GROUP]
+                update = dot1(jnp.concatenate([ah, al, ah], axis=0), jnp.concatenate([rh, rh, rl], axis=0), 0, 0)
                 below = slice(s + STEP, GROUP)
-                left = wa.T[s + STEP :, :]
-                a_ref[g, below, :] = a_ref[g, below, :] - jnp.dot(left, wa, precision=HIGHEST, preferred_element_type=F32)
-                b_ref[g, below, :] = b_ref[g, below, :] - jnp.dot(left, wb, precision=HIGHEST, preferred_element_type=F32)
+                work_ref[g, below] = work_ref[g, below] - update[s + STEP :]
     for g in range(groups):
-        factor_ref[g] = jnp.where(row_of >= lane_of, a_ref[g].T, 0.0)
-        inverse = jnp.where(row_of >= lane_of, b_ref[g], 0.0)
+        factor_ref[g] = jnp.where(row_of >= lane_of, work_ref[g, :, :GROUP].T, 0.0)
+        inverse = jnp.where(row_of >= lane_of, work_ref[g, :, GROUP:], 0.0)
         columns = slice(g * GROUP, (g + 1) * GROUP)
         nh, nl = split(inverse)
         weights = jnp.concatenate([beside(nh, nh), beside(nl, jnp.zeros_like(nl))], axis=0)
@@ -362,7 +378,7 @@
         in_specs=[VMEM_SPEC, VMEM_SPEC, anywhere],
         out_specs=(VMEM_SPEC, VMEM_SPEC, anywhere),
         scratch_shapes=[
-            pltpu.VMEM(gram.shape, F32), pltpu.VMEM(gram.shape, F32), pltpu.VMEM(shape, F32),
+            pltpu.VMEM((groups, GROUP, 2 * GROUP), F32), pltpu.VMEM(shape, F32),
             pltpu.SemaphoreType.DMA(()), pltpu.SemaphoreType.DMA((groups,)),
         ],
         name="factor_and_solve",
@@ -373,13 +389,17 @@
 SLOT_OFFSETS = (0, 1, -2, 2, -1, 3, -3)
 SLOT_ORIGIN = (0, 1, 0, 0, 1, 1, 1)
 CHUNKS = 4
-PIECE = 256
+ROWS = 256
+PIECE = 128
+TICKS = 8
+AHEAD = 2
 BLOCK = 128
+NEAR = 25
 
 
 def apply_kernel(
-    index_ref, present_ref, strips_ref, vector_ref, out_ref,
-    high_ref, low_ref, window, stage_even, stage_odd, image, strip_sem, copy_sem, recv_sem, exit_recv, own_send, relay_send, entry_send,
+    index_ref, strips_ref, vector_ref, out_ref,
+    high_ref, low_ref, window, stage_even, stage_odd, image, strip_sem, copy_sem, entry_recv, recv_sem, exit_recv, own_send, relay_send, entry_send,
     exit_send,
 ):
     blk, rhs = lax.axis_index("blk"), lax.axis_index("rhs")
@@ -402,9 +422,13 @@
     partner = {"blk": blk + sign, "rhs": (1 - x_lo) * 2 + core}
     columns = quarter((x_lo, core)) * (CHUNKS * GROUP)
 
-    def piece(chunk, slot, t):
-        x, c = peer(2 * SLOT_ORIGIN[slot] + t)
-        return window.at[chunk, slot, pl.ds((x * 2 + c) * PIECE, PIECE)]
+    def entry_rows(chunk, n):
+        x, c = peer(n)
+        return window.at[chunk, 0, pl.ds((x * 2 + c) * ROWS, ROWS)]
+
+    def piece(chunk, slot, t, source=None):
+        x, c = peer(2 * SLOT_ORIGIN[slot if source is None else source] + t // 2)
+        return window.at[chunk, slot, pl.ds((x * 2 + c) * ROWS + t % 2 * PIECE, PIECE)]
 
     def remote(src, dst, send, recv, device):
         return pltpu.make_async_remote_copy(
@@ -412,16 +436,17 @@
         )
 
     def strip_copy(i, lane):
-        return pltpu.make_async_copy(strips_ref.at[i], (stage_even, stage_odd)[lane], strip_sem.at[lane])
+        stage = (stage_even, stage_odd)[lane]
+        return pltpu.make_async_copy(strips_ref.at[i], stage.at[pl.ds(0, NEAR)], strip_sem.at[lane])
 
     def own_copy(chunk):
         cols = pl.ds(pl.multiple_of(columns + chunk * GROUP, GROUP), GROUP)
-        return pltpu.make_async_copy(vector_ref.at[:, cols], piece(chunk, 0, 0), copy_sem.at[chunk])
+        return pltpu.make_async_copy(vector_ref.at[:, cols], entry_rows(chunk, 0), copy_sem.at[chunk])
 
     def entry_copy(chunk, t):
         cols = pl.ds(pl.multiple_of(quarter(peer(t)) * (CHUNKS * GROUP) + chunk * GROUP, GROUP), GROUP)
         return remote(
-            vector_ref.at[:, cols], piece(chunk, 0, 0), entry_send.at[chunk, t - 1], recv_sem.at[chunk, 0, t],
+            vector_ref.at[:, cols], entry_rows(chunk, 0), entry_send.at[chunk, t - 1], entry_recv.at[chunk, t - 1],
             group_device(t),
         )
 
@@ -429,21 +454,22 @@
         x, c = peer(t)
         cols = pl.ds(pl.multiple_of(columns + chunk * GROUP, GROUP), GROUP)
         return remote(
-            image.at[chunk, pl.ds((x * 2 + c) * PIECE, PIECE)], out_ref.at[:, cols], exit_send.at[chunk, t - 1],
+            image.at[chunk, pl.ds((x * 2 + c) * ROWS, ROWS)], out_ref.at[:, cols], exit_send.at[chunk, t - 1],
             exit_recv.at[chunk, t - 1], group_device(t),
         )
 
     def send_copy(chunk, t, way):
         slot, device = ((1, partner), (2, ahead), (3, behind))[way]
-        x, c = peer(t)
-        dst = window.at[chunk, slot, pl.ds((x * 2 + c) * PIECE, PIECE)]
-        return remote(piece(chunk, 0, t), dst, own_send.at[chunk, t, way], recv_sem.at[chunk, slot, t], device)
+        return remote(
+            piece(chunk, 0, t), piece(chunk, slot, t, 0), own_send.at[chunk, t, way], recv_sem.at[chunk, slot, t], device
+        )
 
     def relay_copy(chunk, t, way):
         source, slot, device = ((1, 5, behind), (3, 4, partner), (4, 6, ahead))[way]
-        x, c = peer(2 * SLOT_ORIGIN[source] + t)
-        dst = window.at[chunk, slot, pl.ds((x * 2 + c) * PIECE, PIECE)]
-        return remote(piece(chunk, source, t), dst, relay_send.at[chunk, t, way], recv_sem.at[chunk, slot, t], device)
+        return remote(
+            piece(chunk, source, t), piece(chunk, slot, t, source), relay_send.at[chunk, t, way],
+            recv_sem.at[chunk, slot, t], device,
+        )
 
     def arrived(chunk, slot, t):
         at = piece(chunk, slot, t)
@@ -452,8 +478,9 @@
     def send_own(chunk, t):
         if t == 0:
             own_copy(chunk).wait()
-        else:
-            arrived(chunk, 0, t)
+        elif t % 2 == 0:
+            at = entry_rows(chunk, t // 2)
+            remote(at, at, entry_send.at[chunk, 0], entry_recv.at[chunk, t // 2 - 1], partner).wait_recv()
         for way in range(3):
             send_copy(chunk, t, way).start()
 
@@ -469,8 +496,7 @@
         def one_slot(slot, carry):
             for j in range(8):
                 at = slot * 8 + j
-                tile = stage[index_ref[i, at]] * present_ref[i, at]
-                high, low = split(tile)
+                high, low = split(stage[index_ref[i, at]])
                 high_ref[slot, rows, j * BLOCK : (j + 1) * BLOCK] = high
                 low_ref[slot, rows, j * BLOCK : (j + 1) * BLOCK] = low
             return carry
@@ -480,19 +506,15 @@
         if i + 2 < 8:
             strip_copy(i + 2, lane).start()
 
-    def multiply(chunk, first, last):
-        def one(slot, carry):
-            high, low = split(window[chunk, slot])
-            both = dot1(high_ref[slot], beside(high, low), 1, 0)
-            rest = dot1(low_ref[slot], high, 1, 0)
-            image[chunk] = image[chunk] + (both[:, :GROUP] + (both[:, GROUP:] + rest))
-            return carry
-
-        lax.fori_loop(first, last, one, 0)
+    def multiply(chunk, slot):
+        high, low = split(window[chunk, slot])
+        both = dot1(high_ref[slot], beside(high, low), 1, 0)
+        rest = dot1(low_ref[slot], high, 1, 0)
+        image[chunk] = image[chunk] + (both[:, :GROUP] + (both[:, GROUP:] + rest))
 
     def finish(chunk):
         cols = pl.ds(pl.multiple_of(columns + chunk * GROUP, GROUP), GROUP)
-        out_ref[:, cols] = image[chunk, pl.ds(pl.multiple_of(rhs * PIECE, PIECE), PIECE)]
+        out_ref[:, cols] = image[chunk, pl.ds(pl.multiple_of(rhs * ROWS, ROWS), ROWS)]
         for t in (3, 2, 1):
             exit_copy(chunk, t).start()
 
@@ -506,21 +528,23 @@
             else:
                 pl.when(condition)(action)
 
-        if t < 3:
-            when(now, lambda: send_own(chunk, t + 1))
+        if t + AHEAD < TICKS:
+            when(now, lambda: send_own(chunk, t + AHEAD))
         else:
-            when(True if first else chunk + 1 < CHUNKS, lambda: send_own(chunk + 1, 0))
+            when(True if first else chunk + 1 < CHUNKS, lambda: send_own(chunk + 1, t + AHEAD - TICKS))
         for way, lag in ((0, 1), (1, 1), (2, 2)):
             if t >= lag:
                 when(now, functools.partial(relay, chunk, t - lag, way))
             elif not first:
-                relay(back, t - lag + 4, way)
-        if not first:
-            for slot in ((2,), (), (5,), (6,))[t]:
-                for u in range(4):
-                    arrived(back, slot, u)
-            multiply(back, (1, 3, 4, 6)[t], (3, 4, 6, 7)[t])
-            if t == 3:
+                relay(back, t - lag + TICKS, way)
+        if t == TICKS - 1:
+            when(now, lambda: multiply(chunk, 0))
+        elif t and not first:
+            if t in (2, 5, 6):
+                for u in range(TICKS):
+                    arrived(back, t, u)
+            multiply(back, t)
+            if t == SLOTS - 1:
                 finish(back)
 
     for i in range(2):
@@ -536,22 +560,21 @@
     for chunk in range(CHUNKS):
         for t in (2, 3, 1):
             entry_copy(chunk, t).start()
-    send_own(0, 0)
+    for t in range(AHEAD):
+        send_own(0, t)
     image[...] = jnp.zeros_like(image)
-    for t in range(4):
+    for stage in (stage_even, stage_odd):
+        stage[NEAR] = jnp.zeros_like(stage[NEAR])
+    for t in range(TICKS):
+        if t == TICKS - 1:
+            build(t, t % 2)
         tick(0, t, True)
-        for i in (2 * t, 2 * t + 1):
-            build(i, i % 2)
-    multiply(0, 0, 1)
+        if t < TICKS - 1:
+            build(t, t % 2)
 
     def body(chunk, carry):
-        for t in range(4):
+        for t in range(TICKS):
             tick(chunk, t, False)
-
-        @pl.when(chunk < CHUNKS)
-        def _():
-            multiply(chunk, 0, 1)
-
         return carry
 
     lax.fori_loop(1, CHUNKS + 1, body, 0)
@@ -561,7 +584,7 @@
             exit_copy(chunk, t).wait_recv()
             exit_copy(chunk, t).wait_send()
             entry_copy(chunk, t).wait_send()
-        for t in range(4):
+        for t in range(TICKS):
             for way in range(3):
                 send_copy(chunk, t, way).wait_send()
                 relay_copy(chunk, t, way).wait_send()
@@ -570,16 +593,33 @@
     lax.fori_loop(0, CHUNKS, drain, 0)
 
 
+def place_kernel(total, near_ref, index_ref):
+    blocks = near_ref.shape[0]
+    blk = lax.axis_index("blk")
+    sign = 1 - 2 * (blk % 2)
+    at = lax.broadcasted_iota(jnp.int32, index_ref.shape, 1)
+    offset = jnp.zeros(index_ref.shape, jnp.int32)
+    for slot, by in enumerate(SLOT_OFFSETS):
+        offset = jnp.where((at >= slot * blocks) & (at < (slot + 1) * blocks), by * sign * blocks + at - slot * blocks, offset)
+    offset = jnp.where(offset < 0, offset + total, offset)
+    relative = near_ref[...] - blk * blocks
+    relative = jnp.where(relative < 0, relative + total, relative)
+    index = jnp.full(index_ref.shape, NEAR, jnp.int32)
+    for k in range(NEAR):
+        index = jnp.where(relative[:, k : k + 1] == offset, k, index)
+    index_ref[...] = index
+
+
 def apply_near_field(strips, near_cols, vector_block):
     blocks, near = near_cols.shape
     total = blocks * lax.axis_size("blk")
-    blk = lax.axis_index("blk")
-    sign = 1 - 2 * (blk % 2)
-    groups = blk + sign * jnp.array(SLOT_OFFSETS, jnp.int32)
-    target = jnp.mod(groups[:, None] * blocks + jnp.arange(blocks, dtype=jnp.int32)[None], total).reshape(-1)
-    match = near_cols[:, :, None] == target[None, None]
-    index = jnp.sum(jnp.where(match, jnp.arange(near, dtype=jnp.int32)[None, :, None], 0), axis=1)
-    present = jnp.sum(jnp.where(match, 1.0, 0.0), axis=1).astype(F32)
+    index = pl.pallas_call(
+        functools.partial(place_kernel, total),
+        out_shape=jax.ShapeDtypeStruct((blocks, SLOTS * blocks), jnp.int32),
+        in_specs=[VMEM_SPEC],
+        out_specs=VMEM_SPEC,
+        name="place_strips",
+    )(near_cols)
     rows, width = vector_block.shape
     smem = pl.BlockSpec(memory_space=pltpu.SMEM)
     anywhere = pl.BlockSpec(memory_space=pl.ANY)
@@ -588,23 +628,23 @@
     return pl.pallas_call(
         apply_kernel,
         out_shape=jax.ShapeDtypeStruct((rows, width), F32),
-        in_specs=[smem, smem, anywhere, anywhere],
+        in_specs=[smem, anywhere, anywhere],
         out_specs=VMEM_SPEC,
         scratch_shapes=[
             pltpu.VMEM((SLOTS, size, size), BF16),
             pltpu.VMEM((SLOTS, size, size), BF16),
             pltpu.VMEM((CHUNKS, SLOTS, size, GROUP), F32),
-            pltpu.VMEM((near, BLOCK, BLOCK), F32),
-            pltpu.VMEM((near, BLOCK, BLOCK), F32),
+            pltpu.VMEM((near + 1, BLOCK, BLOCK), F32),
+            pltpu.VMEM((near + 1, BLOCK, BLOCK), F32),
             pltpu.VMEM((CHUNKS, size, GROUP), F32),
-            dma((2,)), dma((CHUNKS,)), dma((CHUNKS, SLOTS, 4)), dma((CHUNKS, 3)),
-            dma((CHUNKS, 4, 3)), dma((CHUNKS, 4, 3)), dma((CHUNKS, 3)), dma((CHUNKS, 3)),
+            dma((2,)), dma((CHUNKS,)), dma((CHUNKS, 3)), dma((CHUNKS, SLOTS, TICKS)), dma((CHUNKS, 3)),
+            dma((CHUNKS, TICKS, 3)), dma((CHUNKS, TICKS, 3)), dma((CHUNKS, 3)), dma((CHUNKS, 3)),
         ],
         compiler_params=pltpu.CompilerParams(
             collective_id=3, has_side_effects=True, vmem_limit_bytes=64_000_000
         ),
         name="apply_near_field",
-    )(index, present, strips, vector_block)
+    )(index, strips, vector_block)
 
 
 def local(strips, near_cols, vector_block, basis):

time: 247 us -> 247 us (level)
  Pallas kernels: 243 us -> 246 us
    pallas_call x1, Pallas kernels: 116 us -> 133 us  [apply_near_field(): pl.pallas_call(apply_kernel, out_shape=jax.ShapeDtypeStruct((rows, width)...]
    pallas_call x1, Pallas kernels: 40.9 us -> 25.4 us  [factor_and_solve(): pl.pallas_call(factor_kernel, out_shape=(jax.ShapeDtypeStruct(residual.sh...]
where the time goes in v5:
time: 247 us; the launch traced here: 246 us
  Pallas kernels  246 us (100%)
    pallas_call x1, Pallas kernels, apply_near_field(): pl.pallas_call(apply_kernel, out_shape=jax.ShapeDtypeStruct((rows, width)...  133 us
    pallas_call x1, Pallas kernels, orthogonalize(): pl.pallas_call(orthogonalize_kernel, out_shape=(jax.ShapeDtypeStruct((gro...  85.8 us
    pallas_call x1, Pallas kernels, factor_and_solve(): pl.pallas_call(factor_kernel, out_shape=(jax.ShapeDtypeStruct(residual.sh...  25.4 us

profile of v5, /device:TPU:1, one launch (start us, length us, event | category | flops | bytes accessed | tf_op | source)
XLA Modules:
  0.0 246.4 jit_solution(17506046696083120031)
XLA Ops:
  0.6 1.4 place_strips.1.index_ref
  2.0 132.9 %apply_near_field.1.image_ref = f32[256,2048]{1,0:T(8,128)} custom-call(s32[8,56]{1,0:T(8,128)} %place_strips.1.index_ref, f32[8,25,128,128]{3,2,1,0:T(8,128)} %strips_ref.1, f32[256,2048]{1,0:T(8,128)} %vector_ref.1), custom_call_target="tpu_custom_call" | custom-call | tf_op jit(solution)/shard_map/apply_near_field/pallas_call | solution.py:628
  135.0 85.8 %orthogonalize.1 = (f32[8192,128]{1,0:T(8,128)}, f32[256,2048]{1,0:T(8,128)}, f32[2048,128]{1,0:T(8,128)}) custom-call(f32[4,256,2048]{2,1,0:T(8,128)} %basis_ref.1, f32[256,2048]{1,0:T(8,128)} %apply_near_field.1.image_ref), custom_call_target="tpu_custom_call" | custom-call | tf_op jit(solution)/shard_map/orthogonalize/pallas_call | solution.py:266
  220.8 25.4 %factor_and_solve.1 = (f32[256,2048]{1,0:T(8,128)}, f32[16,128,128]{2,1,0:T(8,128)}, f32[4,16,128,128]{3,2,1,0:T(8,128)}) custom-call(f32[16,128,128]{2,1,0:T(8,128)} %bitcast.3, f32[256,2048]{1,0:T(8,128)} %get-tuple-element.10.residual_ref, f32[16,4,128,128]{3,2,1,0:T(8,128)} %bitcast.2), custom_call_target="tpu_custom_call" | custom-call | tf_op jit(solution)/shard_map/factor_and_solve/pallas_call | solution.py:371

commit v6 on v5

--- a/solution.py
+++ b/solution.py
@@ -390,9 +390,10 @@
 SLOT_ORIGIN = (0, 1, 0, 0, 1, 1, 1)
 CHUNKS = 4
 ROWS = 256
-PIECE = 128
-TICKS = 8
-AHEAD = 2
+PIECE = 256
+TICKS = 4
+AHEAD = 1
+PLAN = ((1, 2), (3,), (4, 5), (6,))
 BLOCK = 128
 NEAR = 25
 
@@ -427,8 +428,8 @@
         return window.at[chunk, 0, pl.ds((x * 2 + c) * ROWS, ROWS)]
 
     def piece(chunk, slot, t, source=None):
-        x, c = peer(2 * SLOT_ORIGIN[slot if source is None else source] + t // 2)
-        return window.at[chunk, slot, pl.ds((x * 2 + c) * ROWS + t % 2 * PIECE, PIECE)]
+        x, c = peer(2 * SLOT_ORIGIN[slot if source is None else source] + t)
+        return window.at[chunk, slot, pl.ds((x * 2 + c) * PIECE, PIECE)]
 
     def remote(src, dst, send, recv, device):
         return pltpu.make_async_remote_copy(
@@ -478,9 +479,9 @@
     def send_own(chunk, t):
         if t == 0:
             own_copy(chunk).wait()
-        elif t % 2 == 0:
-            at = entry_rows(chunk, t // 2)
-            remote(at, at, entry_send.at[chunk, 0], entry_recv.at[chunk, t // 2 - 1], partner).wait_recv()
+        else:
+            at = entry_rows(chunk, t)
+            remote(at, at, entry_send.at[chunk, 0], entry_recv.at[chunk, t - 1], partner).wait_recv()
         for way in range(3):
             send_copy(chunk, t, way).start()
 
@@ -537,15 +538,16 @@
                 when(now, functools.partial(relay, chunk, t - lag, way))
             elif not first:
                 relay(back, t - lag + TICKS, way)
+        if not first:
+            for slot in PLAN[t]:
+                if slot in (2, 5, 6):
+                    for u in range(TICKS):
+                        arrived(back, slot, u)
+                multiply(back, slot)
+                if slot == SLOTS - 1:
+                    finish(back)
         if t == TICKS - 1:
             when(now, lambda: multiply(chunk, 0))
-        elif t and not first:
-            if t in (2, 5, 6):
-                for u in range(TICKS):
-                    arrived(back, t, u)
-            multiply(back, t)
-            if t == SLOTS - 1:
-                finish(back)
 
     for i in range(2):
         strip_copy(i, i).start()
@@ -566,11 +568,14 @@
     for stage in (stage_even, stage_odd):
         stage[NEAR] = jnp.zeros_like(stage[NEAR])
     for t in range(TICKS):
+        rows = range(t * 8 // TICKS, (t + 1) * 8 // TICKS)
         if t == TICKS - 1:
-            build(t, t % 2)
+            for i in rows:
+                build(i, i % 2)
         tick(0, t, True)
         if t < TICKS - 1:
-            build(t, t % 2)
+            for i in rows:
+                build(i, i % 2)
 
     def body(chunk, carry):
         for t in range(TICKS):

time: 247 us -> 231 us (0.935)
  Pallas kernels: 246 us -> 230 us
    pallas_call x1, Pallas kernels: 133 us -> 116 us  [apply_near_field(): pl.pallas_call(apply_kernel, out_shape=jax.ShapeDtypeStruct((rows, width)...]
where the time goes in v6:
time: 231 us; the launch traced here: 230 us
  Pallas kernels  230 us (100%)
    pallas_call x1, Pallas kernels, apply_near_field(): pl.pallas_call(apply_kernel, out_shape=jax.ShapeDtypeStruct((rows, width)...  116 us
    pallas_call x1, Pallas kernels, orthogonalize(): pl.pallas_call(orthogonalize_kernel, out_shape=(jax.ShapeDtypeStruct((gro...  86.4 us
    pallas_call x1, Pallas kernels, factor_and_solve(): pl.pallas_call(factor_kernel, out_shape=(jax.ShapeDtypeStruct(residual.sh...  25.4 us

profile of v6, /device:TPU:1, one launch (start us, length us, event | category | flops | bytes accessed | tf_op | source)
XLA Modules:
  0.0 230.4 jit_solution(2544588140075512493)
XLA Ops:
  0.6 1.4 place_strips.1.index_ref
  2.0 116.4 %apply_near_field.1.image_ref = f32[256,2048]{1,0:T(8,128)} custom-call(s32[8,56]{1,0:T(8,128)} %place_strips.1.index_ref, f32[8,25,128,128]{3,2,1,0:T(8,128)} %strips_ref.1, f32[256,2048]{1,0:T(8,128)} %vector_ref.1), custom_call_target="tpu_custom_call" | custom-call | tf_op jit(solution)/shard_map/apply_near_field/pallas_call | solution.py:633
  118.4 86.4 %orthogonalize.1 = (f32[8192,128]{1,0:T(8,128)}, f32[256,2048]{1,0:T(8,128)}, f32[2048,128]{1,0:T(8,128)}) custom-call(f32[4,256,2048]{2,1,0:T(8,128)} %basis_ref.1, f32[256,2048]{1,0:T(8,128)} %apply_near_field.1.image_ref), custom_call_target="tpu_custom_call" | custom-call | tf_op jit(solution)/shard_map/orthogonalize/pallas_call | solution.py:266
  204.8 25.4 %factor_and_solve.1 = (f32[256,2048]{1,0:T(8,128)}, f32[16,128,128]{2,1,0:T(8,128)}, f32[4,16,128,128]{3,2,1,0:T(8,128)}) custom-call(f32[16,128,128]{2,1,0:T(8,128)} %bitcast.3, f32[256,2048]{1,0:T(8,128)} %get-tuple-element.10.residual_ref, f32[16,4,128,128]{3,2,1,0:T(8,128)} %bitcast.2), custom_call_target="tpu_custom_call" | custom-call | tf_op jit(solution)/shard_map/factor_and_solve/pallas_call | solution.py:371

commit v7 on v6

--- a/solution.py
+++ b/solution.py
@@ -218,23 +218,23 @@
     spans = [(end // depth, last // depth) for end, last in zip(bounds(COEFF_SHARES), bounds(COEFF_SHARES)[1:])]
     swapped = []
     for part, (low, high) in enumerate(spans):
-        lax.fori_loop(low, high, local_coeffs, other_first)
+        lax.fori_loop(low, high, local_coeffs, other_first, unroll=True)
         if part == 0:
             pl.semaphore_wait(barrier, 10)
         swapped.append(swap("coeffs", COEFF_SHARES, coeffs_part, part))
     begun = []
     for part, (low, high) in enumerate(spans):
-        lax.fori_loop(low, high, local_coeffs, own_first)
+        lax.fori_loop(low, high, local_coeffs, own_first, unroll=True)
         begun.append(begin("coeffs", COEFF_SHARES, coeffs_part, part, swapped[part]))
     given = []
     for part in sum_up("coeffs", COEFF_SHARES, begun, coeffs_ref):
         given.append(give(COEFF_SHARES, coeffs_ref, part))
-        lax.fori_loop(*spans[part], local_residual, own_first)
+        lax.fori_loop(*spans[part], local_residual, own_first, unroll=True)
 
     swapped = []
     for part, (low, high) in enumerate(spans):
         given[part].wait_recv()
-        lax.fori_loop(low, high, local_residual, other_first)
+        lax.fori_loop(low, high, local_residual, other_first, unroll=True)
         if part:
             swapped.append(swap("gram", GRAM_SHARES, gram_part, part - 1))
     begun = [begin("gram", GRAM_SHARES, gram_part, part, swapped[part]) for part in range(gram_count)]
@@ -284,10 +284,12 @@
 PIVOTS = 2
 
 
-def factor_kernel(gram_ref, residual_ref, flat_ref, new_ref, factor_ref, coeffs_ref, work_ref, held, in_sem, out_sem):
+def factor_kernel(gram_ref, residual_ref, flat_ref, new_ref, factor_ref, coeffs_ref, work_ref, held, residual, new, in_sem, out_sem):
     groups = gram_ref.shape[0]
-    fetch = pltpu.make_async_copy(flat_ref, held, in_sem)
+    fetch = pltpu.make_async_copy(flat_ref, held, in_sem.at[0])
     fetch.start()
+    bring = pltpu.make_async_copy(residual_ref, residual, in_sem.at[1])
+    bring.start()
     shape = (GROUP, GROUP)
     row_of = lax.broadcasted_iota(jnp.int32, shape, 0)
     lane_of = lax.broadcasted_iota(jnp.int32, shape, 1)
@@ -298,7 +300,7 @@
     lane = lax.broadcasted_iota(jnp.int32, (8, GROUP), 1)
     sub = lax.broadcasted_iota(jnp.int32, (8, GROUP), 0)
     stores = [
-        pltpu.make_async_copy(held.at[g], coeffs_ref.at[:, g], out_sem.at[g]) for g in range(groups)
+        pltpu.make_async_copy(held.at[g], coeffs_ref.at[:, g], out_sem.at[0, g]) for g in range(groups)
     ]
     count = STEP // 8
     for block in range(GROUP // STEP):
@@ -352,14 +354,18 @@
                 update = dot1(jnp.concatenate([ah, al, ah], axis=0), jnp.concatenate([rh, rh, rl], axis=0), 0, 0)
                 below = slice(s + STEP, GROUP)
                 work_ref[g, below] = work_ref[g, below] - update[s + STEP :]
+    bring.wait()
     for g in range(groups):
         factor_ref[g] = jnp.where(row_of >= lane_of, work_ref[g, :, :GROUP].T, 0.0)
         inverse = jnp.where(row_of >= lane_of, work_ref[g, :, GROUP:], 0.0)
         columns = slice(g * GROUP, (g + 1) * GROUP)
         nh, nl = split(inverse)
         weights = jnp.concatenate([beside(nh, nh), beside(nl, jnp.zeros_like(nl))], axis=0)
-        both = dot1(beside(*split(residual_ref[:, columns])), weights, 1, 1)
-        new_ref[:, columns] = both[:, :GROUP] + both[:, GROUP:]
+        both = dot1(beside(*split(residual[:, columns])), weights, 1, 1)
+        new[g] = both[:, :GROUP] + both[:, GROUP:]
+        store = pltpu.make_async_copy(new.at[g], new_ref.at[:, columns], out_sem.at[1, g])
+        store.start()
+        stores.append(store)
     for store in stores:
         store.wait()
 
@@ -375,11 +381,12 @@
             jax.ShapeDtypeStruct(gram.shape, F32),
             jax.ShapeDtypeStruct((count, groups, GROUP, GROUP), F32),
         ),
-        in_specs=[VMEM_SPEC, VMEM_SPEC, anywhere],
-        out_specs=(VMEM_SPEC, VMEM_SPEC, anywhere),
+        in_specs=[VMEM_SPEC, anywhere, anywhere],
+        out_specs=(anywhere, VMEM_SPEC, anywhere),
         scratch_shapes=[
             pltpu.VMEM((groups, GROUP, 2 * GROUP), F32), pltpu.VMEM(shape, F32),
-            pltpu.SemaphoreType.DMA(()), pltpu.SemaphoreType.DMA((groups,)),
+            pltpu.VMEM(residual.shape, F32), pltpu.VMEM((groups, residual.shape[0], GROUP), F32),
+            pltpu.SemaphoreType.DMA((2,)), pltpu.SemaphoreType.DMA((2, groups)),
         ],
         name="factor_and_solve",
     )(gram, residual, flat_coeffs.reshape(shape))

time: 231 us -> 227 us (0.983)
  Pallas kernels: 230 us -> 226 us
where the time goes in v7:
time: 227 us
  Pallas kernels  226 us (100%)
    pallas_call x1, Pallas kernels, apply_near_field(): pl.pallas_call(apply_kernel, out_shape=jax.ShapeDtypeStruct((rows, width)...  116 us
    pallas_call x1, Pallas kernels, orthogonalize(): pl.pallas_call(orthogonalize_kernel, out_shape=(jax.ShapeDtypeStruct((gro...  84.2 us
    pallas_call x1, Pallas kernels, factor_and_solve(): pl.pallas_call(factor_kernel, out_shape=(jax.ShapeDtypeStruct(residual.sh...  24.2 us

profile of v7, /device:TPU:1, one launch (start us, length us, event | category | flops | bytes accessed | tf_op | source)
XLA Modules:
  0.0 226.9 jit_solution(4104071749243049580)
XLA Ops:
  0.6 1.4 place_strips.1.index_ref
  2.0 116.4 %apply_near_field.1.image_ref = f32[256,2048]{1,0:T(8,128)} custom-call(s32[8,56]{1,0:T(8,128)} %place_strips.1.index_ref, f32[8,25,128,128]{3,2,1,0:T(8,128)} %strips_ref.1, f32[256,2048]{1,0:T(8,128)} %vector_ref.1), custom_call_target="tpu_custom_call" | custom-call | tf_op jit(solution)/shard_map/apply_near_field/pallas_call | solution.py:640
  118.4 84.2 %orthogonalize.1 = (f32[8192,128]{1,0:T(8,128)}, f32[256,2048]{1,0:T(8,128)}, f32[2048,128]{1,0:T(8,128)}) custom-call(f32[4,256,2048]{2,1,0:T(8,128)} %basis_ref.1, f32[256,2048]{1,0:T(8,128)} %apply_near_field.1.image_ref), custom_call_target="tpu_custom_call" | custom-call | tf_op jit(solution)/shard_map/orthogonalize/pallas_call | solution.py:266
  202.6 24.2 %factor_and_solve.1 = (f32[256,2048]{1,0:T(8,128)}, f32[16,128,128]{2,1,0:T(8,128)}, f32[4,16,128,128]{3,2,1,0:T(8,128)}) custom-call(f32[16,128,128]{2,1,0:T(8,128)} %bitcast.3, f32[256,2048]{1,0:T(8,128)} %get-tuple-element.10.residual_ref, f32[16,4,128,128]{3,2,1,0:T(8,128)} %bitcast.2), custom_call_target="tpu_custom_call" | custom-call | tf_op jit(solution)/shard_map/factor_and_solve/pallas_call | solution.py:377

commit v8 on v7

--- a/solution.py
+++ b/solution.py
@@ -284,7 +284,7 @@
 PIVOTS = 2
 
 
-def factor_kernel(gram_ref, residual_ref, flat_ref, new_ref, factor_ref, coeffs_ref, work_ref, held, residual, new, in_sem, out_sem):
+def factor_kernel(gram_ref, residual_ref, flat_ref, new_ref, factor_ref, coeffs_ref, work_ref, held, residual, new, factor, in_sem, out_sem):
     groups = gram_ref.shape[0]
     fetch = pltpu.make_async_copy(flat_ref, held, in_sem.at[0])
     fetch.start()
@@ -356,7 +356,10 @@
                 work_ref[g, below] = work_ref[g, below] - update[s + STEP :]
     bring.wait()
     for g in range(groups):
-        factor_ref[g] = jnp.where(row_of >= lane_of, work_ref[g, :, :GROUP].T, 0.0)
+        factor[g] = jnp.where(row_of >= lane_of, work_ref[g, :, :GROUP].T, 0.0)
+        store = pltpu.make_async_copy(factor.at[g], factor_ref.at[g], out_sem.at[2, g])
+        store.start()
+        stores.append(store)
         inverse = jnp.where(row_of >= lane_of, work_ref[g, :, GROUP:], 0.0)
         columns = slice(g * GROUP, (g + 1) * GROUP)
         nh, nl = split(inverse)
@@ -382,11 +385,11 @@
             jax.ShapeDtypeStruct((count, groups, GROUP, GROUP), F32),
         ),
         in_specs=[VMEM_SPEC, anywhere, anywhere],
-        out_specs=(anywhere, VMEM_SPEC, anywhere),
+        out_specs=(anywhere, anywhere, anywhere),
         scratch_shapes=[
             pltpu.VMEM((groups, GROUP, 2 * GROUP), F32), pltpu.VMEM(shape, F32),
             pltpu.VMEM(residual.shape, F32), pltpu.VMEM((groups, residual.shape[0], GROUP), F32),
-            pltpu.SemaphoreType.DMA((2,)), pltpu.SemaphoreType.DMA((2, groups)),
+            pltpu.VMEM(gram.shape, F32), pltpu.SemaphoreType.DMA((2,)), pltpu.SemaphoreType.DMA((3, groups)),
         ],
         name="factor_and_solve",
     )(gram, residual, flat_coeffs.reshape(shape))
@@ -405,9 +408,26 @@
 NEAR = 25
 
 
+def place_strips(near_ref, index_ref, blk, sign):
+    blocks = near_ref.shape[0]
+    total = 32 * blocks
+    at = lax.broadcasted_iota(jnp.int32, index_ref.shape, 1)
+    offset = jnp.zeros(index_ref.shape, jnp.int32)
+    for slot, by in enumerate(SLOT_OFFSETS):
+        here = (at >= slot * blocks) & (at < (slot + 1) * blocks)
+        offset = jnp.where(here, by * sign * blocks + at - slot * blocks, offset)
+    offset = jnp.where(offset < 0, offset + total, offset)
+    relative = near_ref[...] - blk * blocks
+    relative = jnp.where(relative < 0, relative + total, relative)
+    index = jnp.full(index_ref.shape, NEAR, jnp.int32)
+    for k in range(NEAR):
+        index = jnp.where(relative[:, k : k + 1] == offset, k, index)
+    index_ref[...] = index
+
+
 def apply_kernel(
-    index_ref, strips_ref, vector_ref, out_ref,
-    high_ref, low_ref, window, stage_even, stage_odd, image, strip_sem, copy_sem, entry_recv, recv_sem, exit_recv, own_send, relay_send, entry_send,
+    near_ref, strips_ref, vector_ref, out_ref,
+    high_ref, low_ref, window, stage_even, stage_odd, image, index_held, index_ref, index_sem, strip_sem, copy_sem, entry_recv, recv_sem, exit_recv, own_send, relay_send, entry_send,
     exit_send,
 ):
     blk, rhs = lax.axis_index("blk"), lax.axis_index("rhs")
@@ -522,9 +542,20 @@
 
     def finish(chunk):
         cols = pl.ds(pl.multiple_of(columns + chunk * GROUP, GROUP), GROUP)
-        out_ref[:, cols] = image[chunk, pl.ds(pl.multiple_of(rhs * ROWS, ROWS), ROWS)]
-        for t in (3, 2, 1):
-            exit_copy(chunk, t).start()
+        slot = SLOTS - 1
+        high, low = split(window[chunk, slot])
+        halves = beside(high, low)
+        for t in (3, 2, 1, 0):
+            x, c = peer(t)
+            rows = pl.ds(pl.multiple_of((x * 2 + c) * ROWS, ROWS), ROWS)
+            both = dot1(high_ref[slot, rows], halves, 1, 0)
+            rest = dot1(low_ref[slot, rows], high, 1, 0)
+            value = image[chunk, rows] + (both[:, :GROUP] + (both[:, GROUP:] + rest))
+            if t:
+                image[chunk, rows] = value
+                exit_copy(chunk, t).start()
+            else:
+                out_ref[:, cols] = value
 
     def tick(chunk, t, first):
         now = True if first else chunk < CHUNKS
@@ -550,9 +581,10 @@
                 if slot in (2, 5, 6):
                     for u in range(TICKS):
                         arrived(back, slot, u)
-                multiply(back, slot)
                 if slot == SLOTS - 1:
                     finish(back)
+                else:
+                    multiply(back, slot)
         if t == TICKS - 1:
             when(now, lambda: multiply(chunk, 0))
 
@@ -564,6 +596,9 @@
     barrier = pltpu.get_barrier_semaphore()
     for device in [partner, ahead, behind] + [group_device(t) for t in (1, 2, 3)]:
         pl.semaphore_signal(barrier, inc=1, device_id=device, device_id_type=MESH)
+    place_strips(near_ref, index_held, blk, sign)
+    table = pltpu.make_async_copy(index_held, index_ref, index_sem)
+    table.start()
     pl.semaphore_wait(barrier, 6)
 
     for chunk in range(CHUNKS):
@@ -574,6 +609,7 @@
     image[...] = jnp.zeros_like(image)
     for stage in (stage_even, stage_odd):
         stage[NEAR] = jnp.zeros_like(stage[NEAR])
+    table.wait()
     for t in range(TICKS):
         rows = range(t * 8 // TICKS, (t + 1) * 8 // TICKS)
         if t == TICKS - 1:
@@ -605,42 +641,16 @@
     lax.fori_loop(0, CHUNKS, drain, 0)
 
 
-def place_kernel(total, near_ref, index_ref):
-    blocks = near_ref.shape[0]
-    blk = lax.axis_index("blk")
-    sign = 1 - 2 * (blk % 2)
-    at = lax.broadcasted_iota(jnp.int32, index_ref.shape, 1)
-    offset = jnp.zeros(index_ref.shape, jnp.int32)
-    for slot, by in enumerate(SLOT_OFFSETS):
-        offset = jnp.where((at >= slot * blocks) & (at < (slot + 1) * blocks), by * sign * blocks + at - slot * blocks, offset)
-    offset = jnp.where(offset < 0, offset + total, offset)
-    relative = near_ref[...] - blk * blocks
-    relative = jnp.where(relative < 0, relative + total, relative)
-    index = jnp.full(index_ref.shape, NEAR, jnp.int32)
-    for k in range(NEAR):
-        index = jnp.where(relative[:, k : k + 1] == offset, k, index)
-    index_ref[...] = index
-
-
 def apply_near_field(strips, near_cols, vector_block):
     blocks, near = near_cols.shape
-    total = blocks * lax.axis_size("blk")
-    index = pl.pallas_call(
-        functools.partial(place_kernel, total),
-        out_shape=jax.ShapeDtypeStruct((blocks, SLOTS * blocks), jnp.int32),
-        in_specs=[VMEM_SPEC],
-        out_specs=VMEM_SPEC,
-        name="place_strips",
-    )(near_cols)
     rows, width = vector_block.shape
-    smem = pl.BlockSpec(memory_space=pltpu.SMEM)
     anywhere = pl.BlockSpec(memory_space=pl.ANY)
     dma = pltpu.SemaphoreType.DMA
     size = blocks * BLOCK
     return pl.pallas_call(
         apply_kernel,
         out_shape=jax.ShapeDtypeStruct((rows, width), F32),
-        in_specs=[smem, anywhere, anywhere],
+        in_specs=[VMEM_SPEC, anywhere, anywhere],
         out_specs=VMEM_SPEC,
         scratch_shapes=[
             pltpu.VMEM((SLOTS, size, size), BF16),
@@ -649,14 +659,16 @@
             pltpu.VMEM((near + 1, BLOCK, BLOCK), F32),
             pltpu.VMEM((near + 1, BLOCK, BLOCK), F32),
             pltpu.VMEM((CHUNKS, size, GROUP), F32),
-            dma((2,)), dma((CHUNKS,)), dma((CHUNKS, 3)), dma((CHUNKS, SLOTS, TICKS)), dma((CHUNKS, 3)),
+            pltpu.VMEM((blocks, 128), jnp.int32),
+            pltpu.SMEM((blocks, 128), jnp.int32),
+            dma(()), dma((2,)), dma((CHUNKS,)), dma((CHUNKS, 3)), dma((CHUNKS, SLOTS, TICKS)), dma((CHUNKS, 3)),
             dma((CHUNKS, TICKS, 3)), dma((CHUNKS, TICKS, 3)), dma((CHUNKS, 3)), dma((CHUNKS, 3)),
         ],
         compiler_params=pltpu.CompilerParams(
             collective_id=3, has_side_effects=True, vmem_limit_bytes=64_000_000
         ),
         name="apply_near_field",
-    )(index, strips, vector_block)
+    )(near_cols, strips, vector_block)
 
 
 def local(strips, near_cols, vector_block, basis):

time: 227 us -> 225 us (level)
  no operation moved by 1% of the time
where the time goes in v8:
time: 225 us; the launch traced here: 224 us
  Pallas kernels  224 us (100%)
    pallas_call x1, Pallas kernels, apply_near_field(): pl.pallas_call(apply_kernel, out_shape=jax.ShapeDtypeStruct((rows, width)...  116 us
    pallas_call x1, Pallas kernels, orthogonalize(): pl.pallas_call(orthogonalize_kernel, out_shape=(jax.ShapeDtypeStruct((gro...  83.9 us
    pallas_call x1, Pallas kernels, factor_and_solve(): pl.pallas_call(factor_kernel, out_shape=(jax.ShapeDtypeStruct(residual.sh...  23.7 us

profile of v8, /device:TPU:1, one launch (start us, length us, event | category | flops | bytes accessed | tf_op | source)
XLA Modules:
  0.0 224.5 jit_solution(8836332106062514856)
XLA Ops:
  0.6 116.0 %apply_near_field.1.image_ref = f32[256,2048]{1,0:T(8,128)} custom-call(s32[8,25]{1,0:T(8,128)} %near_ref.1, f32[8,25,128,128]{3,2,1,0:T(8,128)} %strips_ref.1, f32[256,2048]{1,0:T(8,128)} %vector_ref.1), custom_call_target="tpu_custom_call" | custom-call | tf_op jit(solution)/shard_map/apply_near_field/pallas_call | solution.py:650
  116.7 83.9 %orthogonalize.1 = (f32[8192,128]{1,0:T(8,128)}, f32[256,2048]{1,0:T(8,128)}, f32[2048,128]{1,0:T(8,128)}) custom-call(f32[4,256,2048]{2,1,0:T(8,128)} %basis_ref.1, f32[256,2048]{1,0:T(8,128)} %apply_near_field.1.image_ref), custom_call_target="tpu_custom_call" | custom-call | tf_op jit(solution)/shard_map/orthogonalize/pallas_call | solution.py:266
  200.6 23.7 %factor_and_solve.1 = (f32[256,2048]{1,0:T(8,128)}, f32[16,128,128]{2,1,0:T(8,128)}, f32[4,16,128,128]{3,2,1,0:T(8,128)}) custom-call(f32[16,128,128]{2,1,0:T(8,128)} %bitcast.3, f32[256,2048]{1,0:T(8,128)} %get-tuple-element.10.residual_ref, f32[16,4,128,128]{3,2,1,0:T(8,128)} %bitcast.2), custom_call_target="tpu_custom_call" | custom-call | tf_op jit(solution)/shard_map/factor_and_solve/pallas_call | solution.py:380

commit v9 on v8

--- a/solution.py
+++ b/solution.py
@@ -567,15 +567,15 @@
             else:
                 pl.when(condition)(action)
 
-        if t + AHEAD < TICKS:
-            when(now, lambda: send_own(chunk, t + AHEAD))
-        else:
-            when(True if first else chunk + 1 < CHUNKS, lambda: send_own(chunk + 1, t + AHEAD - TICKS))
         for way, lag in ((0, 1), (1, 1), (2, 2)):
             if t >= lag:
                 when(now, functools.partial(relay, chunk, t - lag, way))
             elif not first:
                 relay(back, t - lag + TICKS, way)
+        if t + AHEAD < TICKS:
+            when(now, lambda: send_own(chunk, t + AHEAD))
+        else:
+            when(True if first else chunk + 1 < CHUNKS, lambda: send_own(chunk + 1, t + AHEAD - TICKS))
         if not first:
             for slot in PLAN[t]:
                 if slot in (2, 5, 6):

time: 225 us -> 222 us (0.987)
  Pallas kernels: 224 us -> 220 us
where the time goes in v9:
time: 222 us; the launch traced here: 221 us
  Pallas kernels  220 us (99%)
    pallas_call x1, Pallas kernels, apply_near_field(): pl.pallas_call(apply_kernel, out_shape=jax.ShapeDtypeStruct((rows, width)...  115 us
    pallas_call x1, Pallas kernels, orthogonalize(): pl.pallas_call(orthogonalize_kernel, out_shape=(jax.ShapeDtypeStruct((gro...  82.2 us
    pallas_call x1, Pallas kernels, factor_and_solve(): pl.pallas_call(factor_kernel, out_shape=(jax.ShapeDtypeStruct(residual.sh...  23.7 us

profile of v9, /device:TPU:1, one launch (start us, length us, event | category | flops | bytes accessed | tf_op | source)
XLA Modules:
  0.0 221.3 jit_solution(8114456069464934405)
XLA Ops:
  0.6 114.5 %apply_near_field.1.image_ref = f32[256,2048]{1,0:T(8,128)} custom-call(s32[8,25]{1,0:T(8,128)} %near_ref.1, f32[8,25,128,128]{3,2,1,0:T(8,128)} %strips_ref.1, f32[256,2048]{1,0:T(8,128)} %vector_ref.1), custom_call_target="tpu_custom_call" | custom-call | tf_op jit(solution)/shard_map/apply_near_field/pallas_call | solution.py:650
  115.2 82.2 %orthogonalize.1 = (f32[8192,128]{1,0:T(8,128)}, f32[256,2048]{1,0:T(8,128)}, f32[2048,128]{1,0:T(8,128)}) custom-call(f32[4,256,2048]{2,1,0:T(8,128)} %basis_ref.1, f32[256,2048]{1,0:T(8,128)} %apply_near_field.1.image_ref), custom_call_target="tpu_custom_call" | custom-call | tf_op jit(solution)/shard_map/orthogonalize/pallas_call | solution.py:266
  197.4 23.7 %factor_and_solve.1 = (f32[256,2048]{1,0:T(8,128)}, f32[16,128,128]{2,1,0:T(8,128)}, f32[4,16,128,128]{3,2,1,0:T(8,128)}) custom-call(f32[16,128,128]{2,1,0:T(8,128)} %bitcast.3, f32[256,2048]{1,0:T(8,128)} %get-tuple-element.10.residual_ref, f32[16,4,128,128]{3,2,1,0:T(8,128)} %bitcast.2), custom_call_target="tpu_custom_call" | custom-call | tf_op jit(solution)/shard_map/factor_and_solve/pallas_call | solution.py:380
